TPU v7x, 128 devices: a whole 4x4x4 slice. The times are simulated.
128 devices in a mesh: cascade: 2 (over y_lo), coil: 8 (over z, core), readout: 8 (over x, y_hi).
Axes of the slice: x: 4, y: 4 (y_hi: 2, y_lo: 2; y = y_hi * 2 + y_lo), z: 4, core: 2. Of those that a mesh axis runs over, the one named last changes fastest.
Arguments:
- initial: bfloat16 [2, 4, 16, 128, 2, 128], P(None, None, 'readout'), may hold values from -6 to 6
- coil_maps: bfloat16 [2, 16, 16, 128, 2, 128], P(None, 'coil', 'readout'), may hold values from -1.5 to 1.5
- kspace: bfloat16 [2, 16, 4, 16, 128, 2, 128], P(None, 'coil', None, 'readout'), may hold values from -6 to 6
- sampled: int32 [16, 4, 128, 128], P('coil'), may hold values 0 or 1
- first_w: bfloat16 [2, 27, 2, 64], P('cascade'), may hold values from -0.875 to 0.875
- time_w: bfloat16 [2, 3, 64, 64], P('cascade'), may hold values from -0.4375 to 0.4375
- last_w: bfloat16 [2, 27, 64, 2], P('cascade'), may hold values from -0.15625 to 0.15625
Outputs:
- images: bfloat16 [2, 2, 4, 16, 128, 2, 128], P('cascade', None, None, 'readout', 'coil')
Inputs may be any that keep to these rules, and one draw needn't show every extreme that they name: `sampled`: 1 where the sample at that phase, line and partition was acquired for that coil, else 0.
All inputs are finite; a program needn't handle non-finite values. No bound on the sum of `sampled` on one device may be relied on, other than what follows from the above.
Results may differ from a plain program's by a relative error of at most 0.024.
Values may be sent and summed in bfloat16 or wider, within the bound.
A program may use at most 128 MiB of HBM per device.

v0:
```python
import jax
import jax.numpy as jnp
from jax import lax
from jax.sharding import PartitionSpec as P


def extended(block, sides, width):
    for axis, dim in sides:
        count = lax.axis_size(axis)
        forward = [(i, i + 1) for i in range(count - 1)]
        backward = [(target, source) for source, target in forward]
        low = lax.ppermute(
            lax.slice_in_dim(block, block.shape[dim] - width, None, axis=dim), axis, forward
        )
        high = lax.ppermute(lax.slice_in_dim(block, 0, width, axis=dim), axis, backward)
        block = jnp.concatenate([low, block, high], axis=dim)
    return block


def shifted(block, axis, distance):
    devices = range(lax.axis_size(axis))
    route = [(i - distance, i) for i in devices if i - distance in devices]
    return lax.ppermute(block, axis, route)


def fourier_table(length, direction):
    positions = jnp.arange(length, dtype=jnp.int32)
    products = positions[:, None] * positions[None, :] % length
    angles = products.astype(jnp.float32) * (2.0 * jnp.pi / length)
    factor = 1.0 / jnp.sqrt(jnp.float32(length))
    return (jnp.cos(angles) * factor, direction * jnp.sin(angles) * factor)


def row_matrix(length, direction):
    cosine_part, sine_part = fourier_table(length, direction)
    blocks = jnp.stack(
        [jnp.stack([cosine_part, -sine_part], -1), jnp.stack([sine_part, cosine_part], -1)], 1
    )
    return blocks.reshape(2 * length, 2 * length).astype(jnp.bfloat16)


def column_matrix(length, direction):
    cosine_part, sine_part = fourier_table(length, direction)
    blocks = jnp.stack(
        [jnp.stack([cosine_part, sine_part], 1), jnp.stack([-sine_part, cosine_part], 1)], 0
    )
    return blocks.reshape(2 * length, 2 * length).astype(jnp.bfloat16)


def multiply(coil_map, values, conjugate):
    coil_map = coil_map.astype(jnp.float32)
    values = values.astype(jnp.float32)
    map_real, map_imag = (coil_map[..., 0, :], coil_map[..., 1, :])
    value_real, value_imag = (values[..., 0, :], values[..., 1, :])
    if conjugate:
        return jnp.stack(
            [
                map_real * value_real + map_imag * value_imag,
                map_real * value_imag - map_imag * value_real,
            ],
            -2,
        )
    return jnp.stack(
        [
            map_real * value_real - map_imag * value_imag,
            map_real * value_imag + map_imag * value_real,
        ],
        -2,
    )


def along_columns(fields, matrix):
    layout = fields.shape
    flattened = fields.reshape(-1, 2 * layout[-1])
    return jnp.dot(flattened, matrix, preferred_element_type=jnp.float32).reshape(layout)


def along_rows(fields, matrix):
    layout = fields.shape
    flattened = fields.reshape(-1, 2 * layout[-3], layout[-1])
    result = jnp.einsum("ab,nbz->naz", matrix, flattened, preferred_element_type=jnp.float32)
    return result.reshape(layout)


def lift(padded, weights):
    row_count = padded.shape[1] - 2
    line_count = padded.shape[2] - 2
    part_count = padded.shape[4] - 2
    tap_views = [
        padded[
            :,
            row_shift : row_shift + row_count,
            line_shift : line_shift + line_count,
            :,
            part_shift : part_shift + part_count,
        ]
        for row_shift in range(3)
        for line_shift in range(3)
        for part_shift in range(3)
    ]
    stacked = jnp.stack(tap_views, 3)
    stacked = stacked.reshape(stacked.shape[0], row_count, line_count, -1, part_count)
    return jnp.einsum(
        "prlie,io->prloe",
        stacked,
        weights.reshape(-1, weights.shape[-1]),
        preferred_element_type=jnp.float32,
    )


def temporal(hidden, weights):
    phase_count = hidden.shape[0]
    padded = jnp.pad(hidden, ((2, 2), (0, 0), (0, 0), (0, 0), (0, 0)))
    total = hidden.astype(jnp.float32)
    for tap_index in range(3):
        total = total + jnp.einsum(
            "prlie,io->prloe",
            padded[2 * tap_index : 2 * tap_index + phase_count],
            weights[tap_index],
            preferred_element_type=jnp.float32,
        )
    return jax.nn.relu(total).astype(jnp.bfloat16)


def project(edged, weights, base):
    row_count = edged.shape[1] - 2
    line_count = edged.shape[2] - 2
    part_count = edged.shape[4]
    per_tap = jnp.einsum("prlie,tio->prltoe", edged, weights, preferred_element_type=jnp.float32)
    per_tap = jnp.pad(per_tap, ((0, 0), (0, 0), (0, 0), (0, 0), (0, 0), (1, 1)))
    total = base.astype(jnp.float32)
    for row_shift in range(3):
        for line_shift in range(3):
            for part_shift in range(3):
                tap_index = 9 * row_shift + 3 * line_shift + part_shift
                total = (
                    total
                    + per_tap[
                        :,
                        row_shift : row_shift + row_count,
                        line_shift : line_shift + line_count,
                        tap_index,
                        :,
                        part_shift : part_shift + part_count,
                    ]
                )
    return total.astype(jnp.bfloat16)


def cascade(image, coil_maps, measured, sampled, first_w, time_w, last_w, tables):
    forward_rows, forward_columns, inverse_rows, inverse_columns = tables
    coil_image = multiply(coil_maps[:, None], image[None], False).astype(jnp.bfloat16)
    half_done = along_columns(coil_image, forward_columns).astype(jnp.bfloat16)
    spectrum = along_rows(half_done, forward_rows)
    weight = sampled.astype(jnp.float32)[:, :, None, :, None, :]
    mixed = (spectrum + weight * (measured.astype(jnp.float32) - spectrum)).astype(jnp.bfloat16)
    back_half = along_rows(mixed, inverse_rows).astype(jnp.bfloat16)
    restored = along_columns(back_half, inverse_columns)
    terms = jnp.sum(multiply(coil_maps[:, None], restored, True), axis=0)
    summed = lax.psum(terms.astype(jnp.bfloat16), "coil").astype(jnp.float32)
    line_share = summed.shape[2] // lax.axis_size("coil")
    combined = lax.dynamic_slice_in_dim(summed, lax.axis_index("coil") * line_share, line_share, 2)
    combined = combined.astype(jnp.bfloat16)
    padded = extended(combined, (("coil", 2), ("readout", 1)), 1)
    padded = jnp.pad(padded, ((0, 0), (0, 0), (0, 0), (0, 0), (1, 1)))
    hidden = jax.nn.relu(lift(padded, first_w)).astype(jnp.bfloat16)
    mixed_time = temporal(hidden, time_w)
    edged = extended(mixed_time, (("coil", 2), ("readout", 1)), 1)
    return project(edged, last_w, combined)


def per_device(initial, coil_maps, kspace, sampled, first_w, time_w, last_w):
    section_no = lax.axis_index("cascade")
    micro_count = kspace.shape[0]
    line_total = kspace.shape[4]
    part_total = kspace.shape[6]
    tables = (
        row_matrix(line_total, -1.0),
        column_matrix(part_total, -1.0),
        row_matrix(line_total, 1.0),
        column_matrix(part_total, 1.0),
    )
    line_share = line_total // lax.axis_size("coil")
    single = initial[0]
    tick_count = micro_count + lax.axis_size("cascade") - 1
    results = jnp.zeros(
        (1, micro_count, single.shape[0], single.shape[1], line_share, 2, part_total), jnp.bfloat16
    )
    carried = jnp.zeros_like(single)
    for tick_index in range(tick_count):
        position = tick_index - section_no
        valid = (position >= 0) & (position < micro_count)
        picked = jnp.clip(position, 0, micro_count - 1)
        start_image = lax.dynamic_index_in_dim(initial, picked, 0, False)
        image = jnp.where(section_no == 0, start_image, carried)
        block_maps = lax.dynamic_index_in_dim(coil_maps, picked, 0, False)
        block_data = lax.dynamic_index_in_dim(kspace, picked, 0, False)
        output = cascade(
            image, block_maps, block_data, sampled, first_w[0], time_w[0], last_w[0], tables
        )
        updated = lax.dynamic_update_index_in_dim(results, output[None, None], picked, 1)
        results = jnp.where(valid, updated, results)
        if tick_index < tick_count - 1:
            assembled = lax.all_gather(output, "coil", axis=2, tiled=True)
            carried = shifted(assembled, "cascade", 1)
    return results


def solution(mesh):
    in_specs = (
        P(None, None, "readout", None, None, None),
        P(None, "coil", "readout", None, None, None),
        P(None, "coil", None, "readout", None, None, None),
        P("coil", None, None, None),
        P("cascade", None, None, None),
        P("cascade", None, None, None),
        P("cascade", None, None, None),
    )
    out_specs = P("cascade", None, None, "readout", "coil", None, None)
    return jax.shard_map(
        per_device, mesh=mesh, in_specs=in_specs, out_specs=out_specs, check_vma=False
    )
```

profile of v0, /device:TPU:11, one launch (start us, length us, event | category | flops | bytes accessed | tf_op | source)
XLA Modules:
  0.0 703.9 jit_solution(2028351478313013722)
XLA Ops:
  20.0 3.7 constant_dynamic-slice_fusion
  25.4 6.2 copy.131
  31.6 13.1 %reshape.464 = bf16[256,256,1]{1,0,2:T(8,128)(2,1)S(1)} reshape(bf16[128,2,128,2]{3,2,1,0:T(8,128)(2,1)} %copy.131) | data formatting | bytes 262144 | tf_op jit(solution)/shard_map/convert_element_type | solution.py:39
  44.7 6.2 copy.135
  50.9 13.8 %reshape.465 = bf16[256,256,1]{1,0,2:T(8,128)(2,1)} reshape(bf16[128,2,128,2]{3,2,1,0:T(8,128)(2,1)} %copy.135) | data formatting | bytes 262144 | tf_op jit(solution)/shard_map/convert_element_type | solution.py:39
  68.8 3.4 fusion.55
  82.6 61.6 %all-reduce.13.cloned.1.call-done = bf16[4,2,128,2,128]{4,3,2,1,0:T(2,128)(2,1)} async-done(((bf16[4,2,128,2,128]{4,3,2,1,0:T(2,128)(2,1)}), bf16[4,2,128,2,128]{4,3,2,1,0:T(2,128)(2,1)}) %all-reduce.13.cloned.1.call-update) | async-done | bytes 524304 | tf_op jit(solution)/shard_map/psum | solution.py:160
  145.1 3.5 collective-permute-start
  153.8 3.7 collective-permute-start.2
  157.5 4.2 collective-permute-start.3
  171.4 3.4 collective-permute-start.4
  176.8 4.3 collective-permute-done.5
  183.6 4.8 collective-permute-start.6
  191.3 45.9 %collective-permute-done.6 = bf16[4,1,18,64,128]{4,3,2,1,0:T(8,128)(2,1)} collective-permute-done((bf16[4,1,18,64,128]{4,3,2,1,0:T(8,128)(2,1)}, bf16[4,1,18,64,128]{4,3,2,1,0:T(8,128)(2,1)}, u32[]{:S(2)}, u32[]{:S(2)}) %collective-permute-start.6) | collective-permute-done | bytes 1179680 | tf_op jit(solution)/shard_map/ppermute | solution.py:12
  238.8 3.9 fusion.33
  242.7 9.6 %copy.146 = f32[4,4,18,27,2,128]{5,4,2,1,0,3:T(2,128)S(1)} copy(f32[4,4,18,27,2,128]{5,3,4,2,1,0:T(8,128)S(1)} %fusion.33) | data formatting | bytes 15925248 | tf_op jit(solution)/shard_map/prlie,tio->prltoe/transpose | solution.py:129
  252.5 3.5 fusion.229
  256.0 15.4 %all_gather.6 = bf16[4,2,128,2,128]{4,3,2,1,0:T(2,128)(2,1)} all-gather(bf16[4,2,16,2,128]{4,3,2,1,0:T(2,128)(2,1)S(1)} %get-tuple-element.8), channel_id=1, replica_groups=mesh['cascade'=2,'coil'=8,'readout'=8] {'coil'}, dimensions={2}, use_global_device_ids=true | all-gather | bytes 589824 | tf_op jit(solution)/shard_map/all_gather | solution.py:204
  274.8 3.5 fusion.293
  278.2 8.7 %collective-permute-done.8 = bf16[4,2,128,2,128]{4,3,2,1,0:T(2,128)(2,1)} collective-permute-done((bf16[4,2,128,2,128]{4,3,2,1,0:T(2,128)(2,1)}, bf16[4,2,128,2,128]{4,3,2,1,0:T(2,128)(2,1)}, u32[]{:S(2)}, u32[]{:S(2)}) %collective-permute-start.8) | collective-permute-done | bytes 524320 | tf_op jit(solution)/shard_map/ppermute | solution.py:23
  295.2 3.4 fusion.56
  305.7 59.4 %all-reduce.15.cloned.1.call-done = bf16[4,2,128,2,128]{4,3,2,1,0:T(2,128)(2,1)} async-done(((bf16[4,2,128,2,128]{4,3,2,1,0:T(2,128)(2,1)}), bf16[4,2,128,2,128]{4,3,2,1,0:T(2,128)(2,1)}) %all-reduce.15.cloned.1.call-update) | async-done | bytes 524304 | tf_op jit(solution)/shard_map/psum | solution.py:160
  366.0 4.7 collective-permute-start.10
  373.9 3.7 collective-permute-start.11
  377.7 4.1 collective-permute-start.12
  392.0 5.2 collective-permute-start.13
  399.2 4.3 collective-permute-done.14
  405.8 4.8 collective-permute-start.15
  410.6 2.9 collective-permute-start.16
  413.5 45.9 %collective-permute-done.15 = bf16[4,1,18,64,128]{4,3,2,1,0:T(8,128)(2,1)} collective-permute-done((bf16[4,1,18,64,128]{4,3,2,1,0:T(8,128)(2,1)}, bf16[4,1,18,64,128]{4,3,2,1,0:T(8,128)(2,1)}, u32[]{:S(2)}, u32[]{:S(2)}) %collective-permute-start.15) | collective-permute-done | bytes 1179680 | tf_op jit(solution)/shard_map/ppermute | solution.py:12
  461.0 3.8 fusion.9
  464.8 9.6 %copy.238 = f32[4,4,18,128,27,2]{3,5,2,1,0,4:T(2,128)S(1)} copy(f32[4,4,18,128,27,2]{3,4,5,2,1,0:T(8,128)S(1)} %fusion.9) | data formatting | bytes 15925248 | tf_op jit(solution)/shard_map/prlie,tio->prltoe/dot_general | solution.py:129
  474.3 3.5 fusion.230
  478.5 14.4 %all_gather.7 = bf16[4,2,128,2,128]{4,3,2,1,0:T(2,128)(2,1)} all-gather(bf16[4,2,16,2,128]{4,3,2,1,0:T(2,128)(2,1)S(1)} %get-tuple-element.6), channel_id=1, replica_groups=mesh['cascade'=2,'coil'=8,'readout'=8] {'coil'}, dimensions={2}, use_global_device_ids=true | all-gather | bytes 589824 | tf_op jit(solution)/shard_map/all_gather | solution.py:204
  496.0 12.4 %collective-permute-done.17 = bf16[4,2,128,2,128]{4,3,2,1,0:T(2,128)(2,1)} collective-permute-done((bf16[4,2,128,2,128]{4,3,2,1,0:T(2,128)(2,1)}, bf16[4,2,128,2,128]{4,3,2,1,0:T(2,128)(2,1)}, u32[]{:S(2)}, u32[]{:S(2)}) %collective-permute-start.17) | collective-permute-done | bytes 524320 | tf_op jit(solution)/shard_map/ppermute | solution.py:23
  517.7 3.4 fusion.57
  526.0 59.4 %all-reduce.17.cloned.1.call-done = bf16[4,2,128,2,128]{4,3,2,1,0:T(2,128)(2,1)} async-done(((bf16[4,2,128,2,128]{4,3,2,1,0:T(2,128)(2,1)}), bf16[4,2,128,2,128]{4,3,2,1,0:T(2,128)(2,1)}) %all-reduce.17.cloned.1.call-update) | async-done | bytes 524304 | tf_op jit(solution)/shard_map/psum | solution.py:160
  586.4 3.5 collective-permute-start.18
  595.0 3.7 collective-permute-start.20
  598.8 4.2 collective-permute-start.21
  613.1 3.4 collective-permute-start.22
  618.4 4.3 collective-permute-done.23
  624.6 4.8 collective-permute-start.24
  629.4 2.9 collective-permute-start.25
  632.3 45.9 %collective-permute-done.24 = bf16[4,1,18,64,128]{4,3,2,1,0:T(8,128)(2,1)} collective-permute-done((bf16[4,1,18,64,128]{4,3,2,1,0:T(8,128)(2,1)}, bf16[4,1,18,64,128]{4,3,2,1,0:T(8,128)(2,1)}, u32[]{:S(2)}, u32[]{:S(2)}) %collective-permute-start.24) | collective-permute-done | bytes 1179680 | tf_op jit(solution)/shard_map/ppermute | solution.py:12
  679.8 3.5 fusion.18
  683.3 9.6 %copy.237 = f32[4,4,18,128,27,2]{3,5,2,1,0,4:T(2,128)S(1)} copy(f32[4,4,18,128,27,2]{3,4,5,2,1,0:T(8,128)S(1)} %fusion.18) | data formatting | bytes 15925248 | tf_op jit(solution)/shard_map/prlie,tio->prltoe/dot_general | solution.py:129
  692.9 4.0 fusion.231
  (291 shorter events, 131.3 us)
Async XLA Ops:
  6.5 232.3 %copy-start = (bf16[1,27,64,2]{2,3,1,0:T(2,128)(2,1)S(1)}, bf16[1,27,64,2]{2,3,1,0:T(2,128)(2,1)}, u32[]{:S(2)}) copy-start(bf16[1,27,64,2]{2,3,1,0:T(2,128)(2,1)} %param.13) | copy-start | bytes 20740
  6.5 137.7 %all-reduce.13.cloned.1.call-start = ((), (), s32[]{:S(2)}) async-start(), calls=%async_computation | async-start | bytes 1048576 | tf_op jit(solution)/shard_map/psum | solution.py:160
  8.4 4.5 copy-start.14
  18.4 1.6 copy-start.3
  23.7 1.6 copy-start.29
  50.9 13.8 %copy-start.21 = (s32[2,4,128,128]{3,2,1,0:T(8,128)S(1)}, s32[2,4,128,128]{3,2,1,0:T(8,128)}, u32[]{:S(2)}) copy-start(s32[2,4,128,128]{3,2,1,0:T(8,128)} %param.10) | copy-start | bytes 1572868
  81.1 80.6 %copy-start.30 = (bf16[1,27,2,64]{3,2,1,0:T(2,128)(2,1)S(1)}, bf16[1,27,2,64]{3,2,1,0:T(2,128)(2,1)}, u32[]{:S(2)}) copy-start(bf16[1,27,2,64]{3,2,1,0:T(2,128)(2,1)} %param.11) | copy-start | bytes 20740
  82.6 282.5 %all-reduce.15.cloned.1.call-start = ((), (), s32[]{:S(2)}) async-start(), calls=%async_computation.1 | async-start | bytes 1048576 | tf_op jit(solution)/shard_map/psum | solution.py:160
  145.1 6.0 collective-permute-start
  148.7 4.9 collective-permute-start.1
  153.8 8.0 %collective-permute-start.2 = (bf16[4,1,18,2,128]{4,3,2,1,0:T(2,128)(2,1)S(1)}, bf16[4,1,18,2,128]{4,3,2,1,0:T(2,128)(2,1)S(1)}, u32[]{:S(2)}, u32[]{:S(2)}) collective-permute-start(bf16[4,1,18,2,128]{4,3,2,1,0:T(2,128)(2,1)S(1)} %get-tuple-element.61), channel_id=1, source_target_pairs={{0,1},{1,2},{2,3},{3,4},{4,5},{5,6},{6,7},{8,9},{9,10},{10,11},{11... | collective-permute-start | bytes 110600 | tf_op jit(solution)/shard_map/ppermute | solution.py:12
  157.5 6.2 collective-permute-start.3
  161.7 6.5 copy-start.25
  171.4 10.7 %copy-start.1 = (bf16[4,2,16,64,128]{4,3,2,1,0:T(8,128)(2,1)}, bf16[4,2,16,64,128]{4,3,2,1,0:T(8,128)(2,1)S(1)}, u32[]{:S(2)}) copy-start(bf16[4,2,16,64,128]{4,3,2,1,0:T(8,128)(2,1)S(1)} %fusion.32) | copy-start | bytes 6291460
  171.4 5.3 collective-permute-start.4
  174.8 6.3 collective-permute-start.5
  183.6 53.6 %collective-permute-start.6 = (bf16[4,1,18,64,128]{4,3,2,1,0:T(8,128)(2,1)}, bf16[4,1,18,64,128]{4,3,2,1,0:T(8,128)(2,1)}, u32[]{:S(2)}, u32[]{:S(2)}) collective-permute-start(bf16[4,1,18,64,128]{4,3,2,1,0:T(8,128)(2,1)} %get-tuple-element.19), channel_id=1, source_target_pairs={{0,1},{1,2},{2,3},{3,4},{4,5},{5,6},{6,7},{8,9},{9,10},{10,11},{11... | collective-permute-start | bytes 3538952 | tf_op jit(solution)/shard_map/ppermute | solution.py:12
  188.5 50.4 %collective-permute-start.7 = (bf16[4,1,18,64,128]{4,3,2,1,0:T(8,128)(2,1)S(1)}, bf16[4,1,18,64,128]{4,3,2,1,0:T(8,128)(2,1)}, u32[]{:S(2)}, u32[]{:S(2)}) collective-permute-start(bf16[4,1,18,64,128]{4,3,2,1,0:T(8,128)(2,1)S(1)} %get-tuple-element.20), channel_id=1, source_target_pairs={{1,0},{2,1},{3,2},{4,3},{5,4},{6,5},{7,6},{9,8},{10,9},{11,10},{12... | collective-permute-start | bytes 3538952 | tf_op jit(solution)/shard_map/ppermute | solution.py:15
  252.5 20.6 %copy-start.5 = (bf16[1,2,4,2,128,2,128]{6,5,4,3,2,1,0:T(2,128)(2,1)S(1)}, bf16[1,2,4,2,128,2,128]{6,5,4,3,2,1,0:T(2,128)(2,1)}, u32[]{:S(2)}) copy-start(bf16[1,2,4,2,128,2,128]{6,5,4,3,2,1,0:T(2,128)(2,1)} %get-tuple-element.25) | copy-start | bytes 3145732
  256.0 18.8 %copy-start.18 = (bf16[1,2,4,2,16,2,128]{6,5,4,3,2,1,0:T(2,128)(2,1)}, bf16[1,2,4,2,16,2,128]{6,5,4,3,2,1,0:T(2,128)(2,1)S(1)}, u32[]{:S(2)}) copy-start(bf16[1,2,4,2,16,2,128]{6,5,4,3,2,1,0:T(2,128)(2,1)S(1)} %get-tuple-element.7) | copy-start | bytes 393220
  271.4 15.5 %collective-permute-start.8 = (bf16[4,2,128,2,128]{4,3,2,1,0:T(2,128)(2,1)}, bf16[4,2,128,2,128]{4,3,2,1,0:T(2,128)(2,1)}, u32[]{:S(2)}, u32[]{:S(2)}) collective-permute-start(bf16[4,2,128,2,128]{4,3,2,1,0:T(2,128)(2,1)} %all_gather.6), channel_id=1, source_target_pairs={{0,64},{1,65},{2,66},{3,67},{4,68},{5,69},{6,70},{7,71},{8,72},{9,... | collective-permute-start | bytes 1572872 | tf_op jit(solution)/shard_map/ppermute | solution.py:23
  274.7 12.2 %copy-start.15 = (bf16[2,4,2,128,2,128]{5,4,3,2,1,0:T(2,128)(2,1)S(1)}, bf16[2,4,2,128,2,128]{5,4,3,2,1,0:T(2,128)(2,1)}, u32[]{:S(2)}) copy-start(bf16[2,4,2,128,2,128]{5,4,3,2,1,0:T(2,128)(2,1)} %param.7) | copy-start | bytes 3145732
  278.2 11.1 %copy-start.10 = (f32[2,1,2,128,1,128]{5,4,3,2,0,1:T(1,128)}, f32[2,1,2,128,1,128]{5,4,3,2,0,1:T(1,128)S(1)}, u32[]{:S(2)}) copy-start(f32[2,1,2,128,1,128]{5,4,3,2,0,1:T(1,128)S(1)} %get-tuple-element.77) | copy-start | bytes 786436
  278.2 11.2 %copy-start.12 = (f32[2,1,2,128,1,128]{5,4,3,2,0,1:T(1,128)}, f32[2,1,2,128,1,128]{5,4,3,2,0,1:T(1,128)S(1)}, u32[]{:S(2)}) copy-start(f32[2,1,2,128,1,128]{5,4,3,2,0,1:T(1,128)S(1)} %get-tuple-element.78) | copy-start | bytes 786436
  302.3 1.5 copy-start.11
  305.7 279.8 %all-reduce.17.cloned.1.call-start = ((), (), s32[]{:S(2)}) async-start(), calls=%async_computation.2 | async-start | bytes 1048576 | tf_op jit(solution)/shard_map/psum | solution.py:160
  366.0 6.6 collective-permute-start.10
  370.7 3.1 collective-permute-start.9
  373.9 7.9 %collective-permute-start.11 = (bf16[4,1,18,2,128]{4,3,2,1,0:T(2,128)(2,1)S(1)}, bf16[4,1,18,2,128]{4,3,2,1,0:T(2,128)(2,1)S(1)}, u32[]{:S(2)}, u32[]{:S(2)}) collective-permute-start(bf16[4,1,18,2,128]{4,3,2,1,0:T(2,128)(2,1)S(1)} %get-tuple-element.57), channel_id=1, source_target_pairs={{0,1},{1,2},{2,3},{3,4},{4,5},{5,6},{6,7},{8,9},{9,10},{10,11},{11... | collective-permute-start | bytes 110600 | tf_op jit(solution)/shard_map/ppermute | solution.py:12
  377.7 6.2 collective-permute-start.12
  392.0 11.9 %copy-start.2 = (bf16[4,2,16,64,128]{4,3,2,1,0:T(8,128)(2,1)}, bf16[4,2,16,64,128]{4,3,2,1,0:T(8,128)(2,1)S(1)}, u32[]{:S(2)}) copy-start(bf16[4,2,16,64,128]{4,3,2,1,0:T(8,128)(2,1)S(1)} %fusion.30) | copy-start | bytes 6291460
  392.0 7.2 %collective-permute-start.13 = (bf16[4,2,1,64,128]{4,3,2,1,0:T(8,128)(2,1)S(1)}, bf16[4,2,1,64,128]{4,3,2,1,0:T(8,128)(2,1)S(1)}, u32[]{:S(2)}, u32[]{:S(2)}) collective-permute-start(bf16[4,2,1,64,128]{4,3,2,1,0:T(8,128)(2,1)S(1)} %get-tuple-element.26), channel_id=1, source_target_pairs={{0,8},{8,16},{16,24},{24,32},{32,40},{40,48},{48,56},{1,9},{9,17},... | collective-permute-start | bytes 393224 | tf_op jit(solution)/shard_map/ppermute | solution.py:12
  397.3 6.3 collective-permute-start.14
  405.8 53.6 %collective-permute-start.15 = (bf16[4,1,18,64,128]{4,3,2,1,0:T(8,128)(2,1)}, bf16[4,1,18,64,128]{4,3,2,1,0:T(8,128)(2,1)}, u32[]{:S(2)}, u32[]{:S(2)}) collective-permute-start(bf16[4,1,18,64,128]{4,3,2,1,0:T(8,128)(2,1)} %get-tuple-element.17), channel_id=1, source_target_pairs={{0,1},{1,2},{2,3},{3,4},{4,5},{5,6},{6,7},{8,9},{9,10},{10,11},{11... | collective-permute-start | bytes 3538952 | tf_op jit(solution)/shard_map/ppermute | solution.py:12
  410.6 50.4 %collective-permute-start.16 = (bf16[4,1,18,64,128]{4,3,2,1,0:T(8,128)(2,1)}, bf16[4,1,18,64,128]{4,3,2,1,0:T(8,128)(2,1)}, u32[]{:S(2)}, u32[]{:S(2)}) collective-permute-start(bf16[4,1,18,64,128]{4,3,2,1,0:T(8,128)(2,1)} %get-tuple-element.18), channel_id=1, source_target_pairs={{1,0},{2,1},{3,2},{4,3},{5,4},{6,5},{7,6},{9,8},{10,9},{11,10},{12... | collective-permute-start | bytes 3538952 | tf_op jit(solution)/shard_map/ppermute | solution.py:15
  464.7 9.6 %copy-start.19 = (bf16[1,2,4,2,16,2,128]{6,5,4,3,2,1,0:T(2,128)(2,1)S(1)}, bf16[1,2,4,2,16,2,128]{6,5,4,3,2,1,0:T(2,128)(2,1)}, u32[]{:S(2)}) copy-start(bf16[1,2,4,2,16,2,128]{6,5,4,3,2,1,0:T(2,128)(2,1)} %copy-done.18) | copy-start | bytes 393220
  474.3 20.0 %copy-start.4 = (bf16[1,2,4,2,128,2,128]{6,5,4,3,2,1,0:T(2,128)(2,1)S(1)}, bf16[1,2,4,2,128,2,128]{6,5,4,3,2,1,0:T(2,128)(2,1)}, u32[]{:S(2)}) copy-start(bf16[1,2,4,2,128,2,128]{6,5,4,3,2,1,0:T(2,128)(2,1)} %get-tuple-element.23) | copy-start | bytes 3145732
  492.9 15.5 %collective-permute-start.17 = (bf16[4,2,128,2,128]{4,3,2,1,0:T(2,128)(2,1)}, bf16[4,2,128,2,128]{4,3,2,1,0:T(2,128)(2,1)}, u32[]{:S(2)}, u32[]{:S(2)}) collective-permute-start(bf16[4,2,128,2,128]{4,3,2,1,0:T(2,128)(2,1)} %all_gather.7), channel_id=1, source_target_pairs={{0,64},{1,65},{2,66},{3,67},{4,68},{5,69},{6,70},{7,71},{8,72},{9,... | collective-permute-start | bytes 1572872 | tf_op jit(solution)/shard_map/ppermute | solution.py:23
  496.0 15.0 %copy-start.8 = (f32[2,1,2,128,1,128]{5,4,3,2,0,1:T(1,128)S(1)}, f32[2,1,2,128,1,128]{5,4,3,2,0,1:T(1,128)}, u32[]{:S(2)}) copy-start(f32[2,1,2,128,1,128]{5,4,3,2,0,1:T(1,128)} %get-tuple-element.43) | copy-start | bytes 786436
  521.1 2.1 copy-start.17
  586.4 6.0 collective-permute-start.18
  589.9 4.9 collective-permute-start.19
  595.0 8.0 %collective-permute-start.20 = (bf16[4,1,18,2,128]{4,3,2,1,0:T(2,128)(2,1)S(1)}, bf16[4,1,18,2,128]{4,3,2,1,0:T(2,128)(2,1)S(1)}, u32[]{:S(2)}, u32[]{:S(2)}) collective-permute-start(bf16[4,1,18,2,128]{4,3,2,1,0:T(2,128)(2,1)S(1)} %get-tuple-element.53), channel_id=1, source_target_pairs={{0,1},{1,2},{2,3},{3,4},{4,5},{5,6},{6,7},{8,9},{9,10},{10,11},{11... | collective-permute-start | bytes 110600 | tf_op jit(solution)/shard_map/ppermute | solution.py:12
  598.8 6.2 collective-permute-start.21
  613.1 5.3 collective-permute-start.22
  616.5 6.3 collective-permute-start.23
  624.6 53.6 %collective-permute-start.24 = (bf16[4,1,18,64,128]{4,3,2,1,0:T(8,128)(2,1)}, bf16[4,1,18,64,128]{4,3,2,1,0:T(8,128)(2,1)}, u32[]{:S(2)}, u32[]{:S(2)}) collective-permute-start(bf16[4,1,18,64,128]{4,3,2,1,0:T(8,128)(2,1)} %get-tuple-element.15), channel_id=1, source_target_pairs={{0,1},{1,2},{2,3},{3,4},{4,5},{5,6},{6,7},{8,9},{9,10},{10,11},{11... | collective-permute-start | bytes 3538952 | tf_op jit(solution)/shard_map/ppermute | solution.py:12
  629.4 50.4 %collective-permute-start.25 = (bf16[4,1,18,64,128]{4,3,2,1,0:T(8,128)(2,1)S(1)}, bf16[4,1,18,64,128]{4,3,2,1,0:T(8,128)(2,1)}, u32[]{:S(2)}, u32[]{:S(2)}) collective-permute-start(bf16[4,1,18,64,128]{4,3,2,1,0:T(8,128)(2,1)S(1)} %get-tuple-element.16), channel_id=1, source_target_pairs={{1,0},{2,1},{3,2},{4,3},{5,4},{6,5},{7,6},{9,8},{10,9},{11,10},{12... | collective-permute-start | bytes 3538952 | tf_op jit(solution)/shard_map/ppermute | solution.py:15
  (12 other events, 11.1 us)
Sparse Core Ops, SparseCore 0:
  82.7 61.4 all-reduce.12
  305.8 59.2 all-reduce.14
  526.1 59.2 all-reduce.16
where the time goes:
time: 713 us; the launch traced here: 704 us
  waiting for transfers between devices  369 us (52%)
  local copies, waits for them, and re-layouts  132 us (19%)
  starting transfers between devices  86.3 us (12%)
  matrix products  37.7 us (5%)
  other arithmetic  33.6 us (5%)
  blocking collectives  29.8 us (4%)
  between operations  15.2 us (2%)
    psum x3, waiting for transfers between devices, cascade(): summed = lax.psum(terms.astype(jnp.bfloat16), 'coil').astype(jnp.float32)  180 us
    ppermute x12, waiting for transfers between devices, extended(): lax.ppermute(lax.slice_in_dim(block, block.shape[dim] - width, None, axis...  139 us
    ppermute x12, starting transfers between devices, extended(): lax.ppermute(lax.slice_in_dim(block, block.shape[dim] - width, None, axis...  46.7 us
    ppermute x12, starting transfers between devices, extended(): lax.ppermute(lax.slice_in_dim(block, 0, width, axis=dim), axis, backward)  36.3 us
    all_gather x2, blocking collectives, per_device(): assembled = lax.all_gather(output, 'coil', axis=2, tiled=True)  29.8 us
    ppermute x12, waiting for transfers between devices, extended(): lax.ppermute(lax.slice_in_dim(block, 0, width, axis=dim), axis, backward)  28.8 us
    convert_element_type x2, local copies, waits for them, and re-layouts, row_matrix(): return blocks.reshape(2 * length, 2 * length).astype(jnp.bfloat16)  26.9 us
    ppermute x2, waiting for transfers between devices, shifted(): return lax.ppermute(block, axis, route)  21.1 us
  transfers between devices with their start and end apart: 29, of which 20 were waited for; matrix products, arithmetic and copies ran while one was open for 1% of the time, Pallas kernels for 0%

commit v1 on v0

v1 whole, which is shorter than its diff:
```python
import functools

import jax
import jax.numpy as jnp
import numpy as np
from jax import lax
from jax.experimental import pallas as pl
from jax.experimental.pallas import tpu as pltpu
from jax.sharding import PartitionSpec as P

MESH = pl.DeviceIdType.MESH
BF = jnp.bfloat16
F32 = jnp.float32
N = 128
ZS = 4
SHARE = N // ZS
WIN = 40
GROUPS = 9


def complex_blocks(direction):
    k = np.arange(N)
    angle = ((k[:, None] * k[None, :]) % N).astype(np.float32) * np.float32(2.0 * np.pi / N)
    factor = np.float32(1.0 / np.sqrt(N))
    cos, sin = np.cos(angle) * factor, direction * np.sin(angle) * factor
    return np.block([[cos, -sin], [sin, cos]]), np.block([[cos, sin], [-sin, cos]])


def constant_tables():
    rows_forward, cols_forward = complex_blocks(-1.0)
    rows_inverse, cols_inverse = complex_blocks(1.0)
    deint = np.zeros((256, 256))
    for c in range(2):
        for l in range(N):
            deint[c * N + l, 2 * l + c] = 1
    window = np.zeros((2 * ZS * WIN, 256))
    for c in range(2):
        for z in range(ZS):
            for w in range(SHARE + 4):
                l = SHARE * z - 2 + w
                if 0 <= l < N:
                    window[(c * ZS + z) * WIN + w, c * N + l] = 1
    shift = [np.zeros((256, 256)) for _ in range(2)]
    for q in range(2):
        for p in range(N):
            if p > 0:
                shift[0][q * N + p - 1, q * N + p] = 1
            if p < N - 1:
                shift[1][q * N + p + 1, q * N + p] = 1
    slabs = np.zeros((GROUPS * 16, 256))
    for g in range(GROUPS):
        for c in range(2):
            for l8 in range(8):
                slabs[g * 16 + c * 8 + l8, c * WIN + 4 * g + l8] = 1
    base = np.zeros((128, 256))
    gather = np.zeros((128, 256))
    final = np.zeros((128, 256))
    for l in range(SHARE):
        for r in range(2):
            for o in range(2):
                mine = 4 * l + 2 * r + o
                base[mine, r * 2 * WIN + o * WIN + 2 + l] = 1
                gather[(r * 2 + o) * SHARE + l, mine] = 1
                final[((l // 16) * 2 + r) * 32 + (l % 16) * 2 + o, mine] = 1
    return {
        "deint": deint,
        "deint_window": window @ deint,
        "rows_forward": rows_forward,
        "cols_forward": cols_forward,
        "cols_inverse": cols_inverse,
        "rows_inverse": window @ rows_inverse,
        "shift0": shift[0],
        "shift2": shift[1],
        "slabs": slabs,
        "base": base,
        "gather": gather,
        "final": final,
    }


def tables_array():
    tables = constant_tables()
    where, parts, at = {}, [], 0
    for name, table in tables.items():
        where[name] = (at, table.shape[0])
        parts.append(table)
        at += table.shape[0]
    return where, np.concatenate(parts, 0).astype(jnp.bfloat16)


WHERE, TABLES = tables_array()


def first_selection():
    pick = np.zeros((4, 144, 54))
    for j in range(4):
        for a in range(3):
            for e in range(3):
                for c in range(2):
                    for t in range(3):
                        pick[j, ((a * 3 + e) * 2 + c) * 8 + j + t, (9 * a + 3 * t + e) * 2 + c] = 1
    return pick


def last_selection():
    pick = np.zeros((24, 2, 4, 27))
    for delta in range(2):
        for e in range(3):
            for par in range(2):
                for row in range(2):
                    for jpar in range(2):
                        for r4 in range(4):
                            c, a = jpar + 2 * delta - par, r4 - row
                            if 0 <= c < 3 and 0 <= a < 3:
                                pick[((delta * 3 + e) * 2 + par) * 2 + row, jpar, r4, 9 * a + 3 * c + e] = 1
    return pick


def prepared(first_w, time_w, last_w):
    first = jnp.einsum(
        "jkx,xo->jok", jnp.asarray(first_selection(), BF), first_w.reshape(54, 64), preferred_element_type=F32
    )
    first = first.reshape(256, 144).astype(BF)
    turned = jnp.swapaxes(time_w, 1, 2)
    eye, none = jnp.eye(64, dtype=BF), jnp.zeros((64, 64), BF)
    time = jnp.concatenate(
        [
            jnp.concatenate([turned[1], turned[2], eye, none], 1),
            jnp.concatenate([turned[0], turned[1], none, eye], 1),
        ],
        0,
    )
    last = jnp.einsum("mjrt,tio->mojri", jnp.asarray(last_selection(), BF), last_w, preferred_element_type=F32)
    return first, time, last.reshape(48, 512).astype(BF)


def dot(a, b):
    return jnp.dot(a, b, preferred_element_type=F32)


def swap_blocks(x):
    return jnp.concatenate(
        [
            jnp.concatenate([x[:N, :N], x[N:, :N]], 1),
            jnp.concatenate([x[:N, N:], x[N:, N:]], 1),
        ],
        0,
    )


def twice(x):
    return jnp.concatenate([x, x], 1)


def kernel(
    tables_in, initial, coil_maps, kspace, sampled, first_in, time_in, last_in,
    out,
    tab, maps_raw, ksp_raw, img_raw, mask,
    first_s, time_s, last_s,
    maps_d, maps_w, ksp_d, img, acc, rs_send, rs_recv, halo, slab, total, outs,
    local_sem, core_send, core_recv, w_send, w_recv, rs_ssem, rs_rsem, h_ssem, h_rsem,
    ag_ssem, ag_rsem, o_ssem, o_rsem,
):
    cas, coil, ro = lax.axis_index("cascade"), lax.axis_index("coil"), lax.axis_index("readout")
    z, core = coil // 2, coil % 2
    hi = ro % 2
    block = 1 - (hi + cas - 2 * hi * cas)
    other_core = (cas, coil + 1 - 2 * core, ro)
    other_cas = (1 - cas, coil, ro)
    other_both = (1 - cas, coil + 1 - 2 * core, ro)
    peers = [(cas, 2 * ((z + d) % ZS) + core, ro) for d in (1, 2, 3)]
    before, after = (1 - cas, coil, ro - 1), (1 - cas, coil, ro + 1)
    has_before, has_after = ro > 0, ro < 7

    def table(name, columns=256):
        at, count = WHERE[name]
        return tab[at:at + count, :columns]

    def local(number, source, target):
        return pltpu.make_async_copy(source, target, local_sem.at[number])

    def remote(source, target, ssem, rsem, device):
        return pltpu.make_async_remote_copy(
            src_ref=source, dst_ref=target, send_sem=ssem, recv_sem=rsem, device_id=device, device_id_type=MESH
        )

    loads = [
        local(0, tables_in, tab),
        local(1, coil_maps.at[block], maps_raw.at[pl.ds(0, 2)]),
        local(2, kspace.at[block, :, :, core], ksp_raw.at[pl.ds(0, 2)]),
        local(3, sampled.at[:, :, core], mask.at[pl.ds(0, 2)]),
        local(4, initial.at[block, :, core], img_raw),
        local(5, first_in, first_s.at[cas]),
        local(6, time_in, time_s.at[cas]),
        local(7, last_in, last_s.at[cas]),
    ]
    for copy in loads:
        copy.start()

    barrier = pltpu.get_barrier_semaphore()
    for device in [other_core, other_cas, other_both, *peers]:
        pl.semaphore_signal(barrier, inc=1, device_id=device, device_id_type=MESH)

    @pl.when(has_before)
    def _():
        pl.semaphore_signal(barrier, inc=1, device_id=before, device_id_type=MESH)

    @pl.when(has_after)
    def _():
        pl.semaphore_signal(barrier, inc=1, device_id=after, device_id_type=MESH)

    pl.semaphore_wait(barrier, 6 + jnp.where(has_before, 1, 0) + jnp.where(has_after, 1, 0))

    exchange = [
        remote(coil_maps.at[block], maps_raw.at[pl.ds(2, 2)], core_send.at[0], core_recv.at[0], other_core),
        remote(kspace.at[block, :, :, 1 - core], ksp_raw.at[pl.ds(2, 2)], core_send.at[1], core_recv.at[1], other_core),
        remote(sampled.at[:, :, 1 - core], mask.at[pl.ds(2, 2)], core_send.at[2], core_recv.at[2], other_core),
    ]
    for copy in exchange:
        copy.start()
    weights = [
        remote(source, target.at[cas], w_send.at[n], w_recv.at[n], other_cas)
        for n, (source, target) in enumerate(((first_in, first_s), (time_in, time_s), (last_in, last_s)))
    ]
    for copy in weights:
        copy.start()
    weights_in = [
        remote(source, target.at[1 - cas], w_send.at[n], w_recv.at[n], other_cas)
        for n, (source, target) in enumerate(((first_in, first_s), (time_in, time_s), (last_in, last_s)))
    ]

    zero_rows = jnp.zeros((2 * WIN, 256), BF)
    for s in range(2):
        @pl.when(ro == 0)
        def _():
            halo[s, 0] = zero_rows
            halo[s, 1] = zero_rows

        @pl.when(ro == 7)
        def _():
            halo[s, 4] = zero_rows
            halo[s, 5] = zero_rows

    def prepare(j):
        both = jnp.concatenate([maps_raw[j, 0], maps_raw[j, 1]], 1)
        maps_d[j] = dot(table("deint"), both)
        maps_w[j] = dot(table("deint_window"), both)
        for r in range(2):
            pair = jnp.concatenate([ksp_raw[j, 0, r], ksp_raw[j, 1, r]], 1)
            ksp_d[j, r] = swap_blocks(dot(table("deint"), pair)).astype(BF)

    def consistency(s, r, j):
        image = img[s, :, r].astype(F32)
        real, imag = image[:, 0].reshape(N, 256), image[:, 1].reshape(N, 256)
        lanes = slice(r * N, r * N + N)
        map_r, map_i = twice(maps_d[j, :N, lanes]), twice(maps_d[j, N:, lanes])
        coil_image = jnp.concatenate([map_r * real - map_i * imag, map_r * imag + map_i * real], 0).astype(BF)
        half = swap_blocks(dot(table("rows_forward"), coil_image).astype(BF))
        spectrum = dot(half, table("cols_forward"))
        taken = twice(mask[j].reshape(256, N)) != 0
        mixed = jnp.where(taken, ksp_d[j, r].astype(F32), spectrum).astype(BF)
        back = swap_blocks(dot(mixed, table("cols_inverse")).astype(BF))
        restored = dot(table("rows_inverse"), back)
        rows = ZS * WIN
        value_r, value_i = restored[:rows], restored[rows:]
        win_r, win_i = twice(maps_w[j, :rows, lanes]), twice(maps_w[j, rows:, lanes])
        return win_r * value_r + win_i * value_i, win_r * value_i - win_i * value_r

    def reduce_copies(s, r):
        return [
            remote(
                rs_send.at[s, r, (z + d) % ZS], rs_recv.at[s, r, d - 1],
                rs_ssem.at[s, r, d - 1], rs_rsem.at[s, r, d - 1], peers[d - 1],
            )
            for d in (1, 2, 3)
        ]

    def data_consistency(s, r):
        rows = ZS * WIN

        def pair(jp, unused):
            if s == 0 and r == 0:
                @pl.when(jp == 1)
                def _():
                    for copy in exchange:
                        copy.wait_recv()
                    prepare(2)
                    prepare(3)
            first_r, first_i = consistency(s, r, 2 * jp)
            second_r, second_i = consistency(s, r, 2 * jp + 1)
            acc[:rows] += first_r + second_r
            acc[rows:] += first_i + second_i
            return unused

        acc[...] = jnp.zeros_like(acc)
        lax.fori_loop(0, 2, pair, 0)
        for share in range(ZS):
            at = share * WIN
            rs_send[s, r, share] = jnp.concatenate(
                [acc[at:at + WIN], acc[rows + at:rows + at + WIN]], 0
            ).astype(BF)
        for copy in reduce_copies(s, r):
            copy.start()

    def halo_copies(s, r):
        return (
            remote(halo.at[s, 2 + r], halo.at[s, 4 + r], h_ssem.at[s, r, 0], h_rsem.at[s, r, 0], before),
            remote(halo.at[s, 2 + r], halo.at[s, r], h_ssem.at[s, r, 1], h_rsem.at[s, r, 1], after),
        )

    def combine(s, r):
        for copy in reduce_copies(s, r):
            copy.wait_recv()
        summed = rs_send[s, r, z].astype(F32)
        for d in range(3):
            summed = summed + rs_recv[s, r, d].astype(F32)
        halo[s, 2 + r] = summed.astype(BF)
        to_before, to_after = halo_copies(s, r)

        @pl.when(has_before)
        def _():
            to_before.start()

        @pl.when(has_after)
        def _():
            to_after.start()

    def denoise(s):
        for r in range(2):
            to_before, to_after = halo_copies(s, r)

            @pl.when(has_after)
            def _():
                to_before.wait_recv()

            @pl.when(has_before)
            def _():
                to_after.wait_recv()

        cells = halo[s].reshape(6 * 2 * WIN, 256)
        for e in range(3):
            moved = cells if e == 1 else dot(cells, table(f"shift{e}")).astype(BF)
            for row in range(6):
                piece = moved[row * 2 * WIN:(row + 1) * 2 * WIN]
                parts = dot(table("slabs", 2 * WIN), piece).astype(BF)
                at = (row * 3 + e) * 16
                for g in range(GROUPS):
                    slab[g, at:at + 16] = parts[16 * g:16 * g + 16]

        if s == 0:
            @pl.when(cas == 1)
            def _():
                for copy in weights_in:
                    copy.wait_recv()
        else:
            @pl.when(cas == 0)
            def _():
                for copy in weights_in:
                    copy.wait_recv()

        row_of = (lax.broadcasted_iota(jnp.int32, (48, 512), 1) // 64) % 4
        dead = ((row_of == 0) & (ro == 0)) | ((row_of == 3) & (ro == 7))
        last = jnp.where(dead, 0.0, last_s[s].astype(F32))
        total[...] = jnp.zeros_like(total)

        def group(g, unused):
            features = []
            for row in range(4):
                hidden = dot(first_s[s], slab[g, 48 * row:48 * row + 144])
                hidden = jnp.maximum(hidden, 0.0).astype(BF)
                for u in range(2):
                    lines = []
                    for j in (2 * u, 2 * u + 1):
                        one = hidden[64 * j:64 * j + 64]
                        lines.append(jnp.concatenate([one[:, :N], one[:, N:]], 0))
                    lines = jnp.concatenate(lines, 1)
                    mixed = dot(time_s[s], jnp.concatenate([lines, lines], 0))
                    features.append(jnp.maximum(mixed, 0.0).astype(BF))
            for u in range(2):
                k = 2 * g + u
                stack = []
                for j in range(2):
                    for row in range(4):
                        one = features[2 * row + u][:, j * N:j * N + N]
                        stack.append(jnp.concatenate([one[:64], one[64:]], 1))
                stack = jnp.concatenate(stack, 0)
                keep0 = jnp.where((k == 0) & (z == 0), 0.0, 1.0)
                keep1 = jnp.where((k == 16) & (z == ZS - 1), 0.0, 1.0)
                weight = jnp.concatenate([last[:, :256] * keep0, last[:, 256:] * keep1], 1).astype(BF)
                result = dot(weight, stack)
                total[k + 1] += result[:24]
                total[k] += result[24:]
            return unused

        lax.fori_loop(0, GROUPS, group, 0)

        taps = [total[1:17, 8 * e:8 * e + 8].reshape(128, 256) for e in range(3)]
        lane = lax.broadcasted_iota(jnp.int32, (128, N), 1)
        halves = []
        for q in range(2):
            at = slice(q * N, q * N + N)
            low = jnp.where(lane == 0, 0.0, pltpu.roll(taps[0][:, at], 1, 1))
            high = jnp.where(lane == N - 1, 0.0, pltpu.roll(taps[2][:, at], N - 1, 1))
            halves.append(low + taps[1][:, at] + high)
        own = jnp.concatenate([halo[s, 2], halo[s, 3]], 0)
        return (dot(table("base", 4 * WIN), own) + jnp.concatenate(halves, 1)).astype(BF)

    def gather_copies(arriving):
        return [
            remote(
                img.at[1, z], img.at[1, (z + ZS - d) % ZS if arriving else z],
                ag_ssem.at[d - 1], ag_rsem.at[d - 1], peers[d - 1],
            )
            for d in (1, 2, 3)
        ]

    def keep_output(s, image):
        ordered = dot(table("final", 128), image).astype(BF)
        for half in range(2):
            for q in range(2):
                for r in range(2):
                    at = (half * 2 + r) * 32
                    outs[s, half, q, r] = ordered[at:at + 32, q * N:q * N + N]

    def near_copies(s):
        return (
            local(8, outs.at[s, core], out.at[block, :, core]),
            remote(outs.at[s, 1 - core], out.at[block, :, core], o_ssem.at[0], o_rsem.at[0], other_core),
        )

    def far_copies(s):
        return (
            remote(outs.at[s, core], out.at[block, :, core], o_ssem.at[1], o_rsem.at[1], other_cas),
            remote(outs.at[s, 1 - core], out.at[block, :, core], o_ssem.at[2], o_rsem.at[2], other_both),
        )

    def send_output(s):
        @pl.when(cas == s)
        def _():
            for copy in near_copies(s):
                copy.start()

        @pl.when(cas != s)
        def _():
            for copy in far_copies(s):
                copy.start()

    for copy in loads[:5]:
        copy.wait()
    for r in range(2):
        pair = jnp.concatenate([img_raw[0, r], img_raw[1, r]], 1)
        plain = dot(table("deint"), pair).astype(BF)
        for share in range(ZS):
            for c in range(2):
                at = c * N + share * SHARE
                img[0, share, r, c] = plain[at:at + SHARE]
    prepare(0)
    prepare(1)
    for copy in loads[5:]:
        copy.wait()

    for s in range(2):
        data_consistency(s, 0)
        data_consistency(s, 1)
        combine(s, 0)
        combine(s, 1)
        image = denoise(s)
        if s == 0:
            shares = dot(table("gather", 128), image).astype(BF)
            for r in range(2):
                for c in range(2):
                    at = (2 * r + c) * SHARE
                    img[1, z, r, c] = shares[at:at + SHARE]
            for copy in gather_copies(False):
                copy.start()
        keep_output(s, image)
        send_output(s)
        if s == 0:
            for copy in gather_copies(True):
                copy.wait_recv()

    for copy in exchange + weights + gather_copies(False):
        copy.wait_send()
    for s in range(2):
        for r in range(2):
            for copy in reduce_copies(s, r):
                copy.wait_send()
            to_before, to_after = halo_copies(s, r)

            @pl.when(has_before)
            def _():
                to_before.wait_send()

            @pl.when(has_after)
            def _():
                to_after.wait_send()

        @pl.when(cas == s)
        def _():
            keep, give = near_copies(s)
            keep.wait()
            give.wait_send()

        @pl.when(cas != s)
        def _():
            for copy in far_copies(s):
                copy.wait_send()

    arriving = (
        remote(outs.at[0, 0], out.at[block, :, 1 - core], o_ssem.at[0], o_rsem.at[0], other_core),
        remote(outs.at[0, 0], out.at[1 - block, :, core], o_ssem.at[1], o_rsem.at[1], other_cas),
        remote(outs.at[0, 0], out.at[1 - block, :, 1 - core], o_ssem.at[2], o_rsem.at[2], other_both),
    )
    for copy in arriving:
        copy.wait_recv()


def per_device(initial, coil_maps, kspace, sampled, first_w, time_w, last_w):
    first, time, last = prepared(first_w[0], time_w[0], last_w[0])
    dma = pltpu.SemaphoreType.DMA
    out = pl.pallas_call(
        kernel,
        out_shape=jax.ShapeDtypeStruct((2, 2, 2, 2, 32, N), BF),
        in_specs=[pl.BlockSpec(memory_space=pl.ANY)] * 8,
        out_specs=pl.BlockSpec(memory_space=pl.ANY),
        scratch_shapes=[
            pltpu.VMEM(TABLES.shape, BF),
            pltpu.VMEM((4, 2, 256, N), BF),
            pltpu.VMEM((4, 2, 2, 256, N), BF),
            pltpu.VMEM((2, 2, 256, N), BF),
            pltpu.VMEM((4, 2, N, N), jnp.int32),
            pltpu.VMEM((2, 256, 144), BF),
            pltpu.VMEM((2, 128, 256), BF),
            pltpu.VMEM((2, 48, 512), BF),
            pltpu.VMEM((4, 256, 256), F32),
            pltpu.VMEM((4, 2 * ZS * WIN, 256), F32),
            pltpu.VMEM((4, 2, 256, 256), BF),
            pltpu.VMEM((2, ZS, 2, 2, SHARE, 256), BF),
            pltpu.VMEM((2 * ZS * WIN, 256), F32),
            pltpu.VMEM((2, 2, ZS, 2 * WIN, 256), BF),
            pltpu.VMEM((2, 2, 3, 2 * WIN, 256), BF),
            pltpu.VMEM((2, 6, 2 * WIN, 256), BF),
            pltpu.VMEM((GROUPS, 288, 256), BF),
            pltpu.VMEM((20, 24, 256), F32),
            pltpu.VMEM((2, 2, 2, 2, 32, N), BF),
            dma((9,)),
            dma((3,)),
            dma((3,)),
            dma((3,)),
            dma((3,)),
            dma((2, 2, 3)),
            dma((2, 2, 3)),
            dma((2, 2, 2)),
            dma((2, 2, 2)),
            dma((3,)),
            dma((3,)),
            dma((3,)),
            dma((3,)),
        ],
        compiler_params=pltpu.CompilerParams(
            collective_id=0, has_side_effects=True, vmem_limit_bytes=48 * 1024 * 1024
        ),
    )(
        jnp.asarray(TABLES),
        initial.reshape(2, 2, 2, 2, 256, N),
        coil_maps.reshape(2, 2, 2, 256, N),
        kspace.reshape(2, 2, 2, 2, 2, 256, N),
        sampled.reshape(2, 2, 2, N, N),
        first,
        time,
        last,
    )
    return out.reshape(1, 2, 4, 2, 16, 2, N)


def solution(mesh):
    in_specs = (
        P(None, None, "readout", None, None, None),
        P(None, "coil", "readout", None, None, None),
        P(None, "coil", None, "readout", None, None, None),
        P("coil", None, None, None),
        P("cascade", None, None, None),
        P("cascade", None, None, None),
        P("cascade", None, None, None),
    )
    out_specs = P("cascade", None, None, "readout", "coil", None, None)
    return jax.shard_map(per_device, mesh=mesh, in_specs=in_specs, out_specs=out_specs, check_vma=False)
```

time: 713 us -> 70.3 us (0.10); the launches traced: 704 us -> 69.7 us
  waiting for transfers between devices: 369 us -> 0 us
  local copies, waits for them, and re-layouts: 132 us -> 9.42 us
  starting transfers between devices: 86.3 us -> 0 us
  Pallas kernels: 0 us -> 58 us
  matrix products: 37.7 us -> 2.08 us
  other arithmetic: 33.6 us -> 0.11 us
  blocking collectives: 29.8 us -> 0 us
  between operations: 15.2 us -> 0.07 us
    ppermute x26 -> x0, waiting for transfers between devices: 189 us -> none  [the longest x12 139 us: extended(): lax.ppermute(lax.slice_in_dim(block, block.shape[dim] - width, None, axis...]
    psum x3 -> x0, waiting for transfers between devices: 180 us -> none  [cascade(): summed = lax.psum(terms.astype(jnp.bfloat16), 'coil').astype(jnp.float32)]
    ppermute x26 -> x0, starting transfers between devices: 86.2 us -> none  [the longest x12 46.7 us: extended(): lax.ppermute(lax.slice_in_dim(block, block.shape[dim] - width, None, axis...]
    pallas_call x0 -> x1, Pallas kernels: none -> 58 us  [per_device(): pl.pallas_call(kernel, out_shape=jax.ShapeDtypeStruct((2, 2, 2, 2, 32, N)...]
    convert_element_type x17 -> x2, local copies, waits for them, and re-layouts: 48.5 us -> 0.17 us  [prepared(): return (first, time, last.reshape(48, 512).astype(BF))]
    dot_general x24 -> x2, matrix products: 37.7 us -> 2.08 us  [the longest x1 1.12 us: prepared(): jnp.einsum('jkx,xo->jok', jnp.asarray(first_selection(), BF), first_w.res...]
    all_gather x2 -> x0, blocking collectives: 29.8 us -> none  [per_device(): assembled = lax.all_gather(output, 'coil', axis=2, tiled=True)]
    dot_general x4 -> x0, local copies, waits for them, and re-layouts: 20.9 us -> none  [the longest x2 19.1 us: project(): jnp.einsum('prlie,tio->prltoe', edged, weights, preferred_element_type=jn...]
  transfers between devices with their start and end apart: 29 -> 0, of which waited for: 20 -> 0; matrix products, arithmetic and copies ran while one was open for 1% -> 0% of each run, Pallas kernels for 0% -> 0%
where the time goes in v1:
time: 70.3 us; the launch traced here: 69.7 us
  Pallas kernels  58 us (83%)
  local copies, waits for them, and re-layouts  9.42 us (13%)
  matrix products  2.08 us (3%)
    pallas_call x1, Pallas kernels, per_device(): pl.pallas_call(kernel, out_shape=jax.ShapeDtypeStruct((2, 2, 2, 2, 32, N)...  58 us
    unnamed x14, local copies, waits for them, and re-layouts  8.49 us

profile of v1, /device:TPU:11, one launch (start us, length us, event | category | flops | bytes accessed | tf_op | source)
XLA Modules:
  0.0 69.7 jit_solution(3830373916444229959)
XLA Ops:
  0.0 0.0 copy-start
  0.0 0.7 %copy-done = bf16[1,27,64,2]{2,3,1,0:T(2,128)(2,1)S(1)} copy-done((bf16[1,27,64,2]{2,3,1,0:T(2,128)(2,1)S(1)}, bf16[1,27,64,2]{2,3,1,0:T(2,128)(2,1)}, u32[]{:S(2)}) %copy-start) | copy-done | bytes 6936
  0.7 0.7 %reshape.24 = bf16[54,64,1]{1,0,2:T(8,128)(2,1)S(1)} reshape(bf16[1,27,2,64]{3,2,1,0:T(2,128)(2,1)} %param.14) | data formatting | bytes 13824 | tf_op jit(solution)/shard_map/reshape;squeeze | solution.py:121
  1.5 0.9 %copy.11 = bf16[1,3,64,64]{2,3,1,0:T(8,128)(2,1)S(1)} copy(bf16[1,3,64,64]{3,2,1,0:T(8,128)(2,1)} %param.15) | data formatting | bytes 49152 | tf_op args[5]
  2.4 0.1 maximum_maximum_fusion.time_in
  2.5 1.0 %fusion = bf16[24,2,2,4,64]{4,0,1,3,2:T(8,128)(2,1)S(1)} fusion(bf16[24,2,4,27,1]{3,0,4,2,1:T(8,128)(2,1)} %constant.18, bf16[27,64,2,1,1]{1,2,0,4,3:T(2,128)(2,1)S(1)} %bitcast.28), kind=kOutput, calls=%fused_computation.2 | convolution fusion | flops 1351680 | bytes 66432 | tf_op jit(solution)/shard_map/mjrt,tio->mojri/dot_general | solution.py:133
  3.5 0.1 convert_element_type.25.last_in
  3.6 1.1 %convolution_convert_fusion = bf16[4,144,64]{1,2,0:T(8,128)(2,1)S(1)} fusion(bf16[4,144,54]{1,2,0:T(8,128)(2,1)} %constant.8.clone, bf16[54,64,1]{1,0,2:T(8,128)(2,1)S(1)} %reshape.24), kind=kOutput, calls=%fused_computation | convolution fusion | flops 4018176 | bytes 142848 | tf_op jit(solution)/shard_map/jkx,xo->jok/dot_general | solution.py:120
  4.8 0.0 copy-start.1
  4.8 1.6 %copy-done.1 = bf16[2,2,4,2,128,2,128]{6,5,4,3,2,1,0:T(2,128)(2,1)S(1)} copy-done((bf16[2,2,4,2,128,2,128]{6,5,4,3,2,1,0:T(2,128)(2,1)S(1)}, bf16[2,2,4,2,128,2,128]{6,5,4,3,2,1,0:T(2,128)(2,1)}, u32[]{:S(2)}) %copy-start.1) | copy-done | bytes 2097176
  6.4 0.0 copy-start.2
  6.4 1.3 %copy-done.2 = bf16[2704,256]{1,0:T(8,128)(2,1)S(1)} copy-done((bf16[2704,256]{1,0:T(8,128)(2,1)S(1)}, bf16[2704,256]{1,0:T(8,128)(2,1)}, u32[]{:S(2)}) %copy-start.2) | copy-done | bytes 1384472
  7.7 0.0 copy-start.3
  7.7 1.2 %copy-done.3 = bf16[2,4,2,128,2,128]{5,4,3,2,1,0:T(2,128)(2,1)S(1)} copy-done((bf16[2,4,2,128,2,128]{5,4,3,2,1,0:T(2,128)(2,1)S(1)}, bf16[2,4,2,128,2,128]{5,4,3,2,1,0:T(2,128)(2,1)}, u32[]{:S(2)}) %copy-start.3) | copy-done | bytes 1048600
  8.9 0.0 copy-start.4
  8.9 1.0 %copy-done.4 = bf16[2,2,2,128,2,128]{5,4,3,2,1,0:T(2,128)(2,1)S(1)} copy-done((bf16[2,2,2,128,2,128]{5,4,3,2,1,0:T(2,128)(2,1)S(1)}, bf16[2,2,2,128,2,128]{5,4,3,2,1,0:T(2,128)(2,1)}, u32[]{:S(2)}) %copy-start.4) | copy-done | bytes 524312
  10.0 0.0 copy-start.5
  10.0 1.0 %copy-done.5 = s32[2,4,128,128]{3,2,1,0:T(8,128)S(1)} copy-done((s32[2,4,128,128]{3,2,1,0:T(8,128)S(1)}, s32[2,4,128,128]{3,2,1,0:T(8,128)}, u32[]{:S(2)}) %copy-start.5) | copy-done | bytes 524312
  11.0 58.0 %shard_map.100 = bf16[2,2,2,2,32,128]{5,4,3,2,1,0:T(8,128)(2,1)S(1)} custom-call(bf16[2704,256]{1,0:T(8,128)(2,1)S(1)} %copy-done.2, bf16[2,2,2,2,256,128]{5,4,3,2,1,0:T(8,128)(2,1)S(1)} %bitcast.30, bf16[2,2,2,256,128]{4,3,2,1,0:T(8,128)(2,1)S(1)} %bitcast.31, bf16[2,2,2,2,2,256,128]{6,5,4,3,2,1,0:T(8,128)(2,1)S(1)} %bitcast.29, ...), custom_call_target="tpu_custom_call" | custom-call | tf_op jit(solution)/shard_map/pallas_call | solution.py:521
  69.1 0.7 copy.21
  (4 shorter events, 0.1 us)
Async XLA Ops:
  0.0 0.7 %copy-start = (bf16[1,27,64,2]{2,3,1,0:T(2,128)(2,1)S(1)}, bf16[1,27,64,2]{2,3,1,0:T(2,128)(2,1)}, u32[]{:S(2)}) copy-start(bf16[1,27,64,2]{2,3,1,0:T(2,128)(2,1)} %param.16) | copy-start | bytes 20740
  4.8 1.6 %copy-start.1 = (bf16[2,2,4,2,128,2,128]{6,5,4,3,2,1,0:T(2,128)(2,1)S(1)}, bf16[2,2,4,2,128,2,128]{6,5,4,3,2,1,0:T(2,128)(2,1)}, u32[]{:S(2)}) copy-start(bf16[2,2,4,2,128,2,128]{6,5,4,3,2,1,0:T(2,128)(2,1)} %param.12) | copy-start | bytes 6291460
  6.4 1.3 %copy-start.2 = (bf16[2704,256]{1,0:T(8,128)(2,1)S(1)}, bf16[2704,256]{1,0:T(8,128)(2,1)}, u32[]{:S(2)}) copy-start(bf16[2704,256]{1,0:T(8,128)(2,1)} %constant.10.clone.tables_in) | copy-start | bytes 4153348
  7.7 1.2 %copy-start.3 = (bf16[2,4,2,128,2,128]{5,4,3,2,1,0:T(2,128)(2,1)S(1)}, bf16[2,4,2,128,2,128]{5,4,3,2,1,0:T(2,128)(2,1)}, u32[]{:S(2)}) copy-start(bf16[2,4,2,128,2,128]{5,4,3,2,1,0:T(2,128)(2,1)} %param.10) | copy-start | bytes 3145732
  8.9 1.0 %copy-start.4 = (bf16[2,2,2,128,2,128]{5,4,3,2,1,0:T(2,128)(2,1)S(1)}, bf16[2,2,2,128,2,128]{5,4,3,2,1,0:T(2,128)(2,1)}, u32[]{:S(2)}) copy-start(bf16[2,2,2,128,2,128]{5,4,3,2,1,0:T(2,128)(2,1)} %param.11) | copy-start | bytes 1572868
  10.0 1.0 %copy-start.5 = (s32[2,4,128,128]{3,2,1,0:T(8,128)S(1)}, s32[2,4,128,128]{3,2,1,0:T(8,128)}, u32[]{:S(2)}) copy-start(s32[2,4,128,128]{3,2,1,0:T(8,128)} %param.13) | copy-start | bytes 1572868

commit v2 on v1

--- a/solution.py
+++ b/solution.py
@@ -24,6 +24,33 @@
     factor = np.float32(1.0 / np.sqrt(N))
     cos, sin = np.cos(angle) * factor, direction * np.sin(angle) * factor
     return np.block([[cos, -sin], [sin, cos]]), np.block([[cos, sin], [-sin, cos]])
+
+
+def first_selection():
+    pick = np.zeros((4, 64, 144))
+    for j in range(4):
+        for a in range(3):
+            for e in range(3):
+                for c in range(2):
+                    for t in range(3):
+                        pick[j, (9 * a + 3 * t + e) * 2 + c, ((a * 3 + e) * 2 + c) * 8 + j + t] = 1
+    return pick
+
+
+def last_selection():
+    pick = np.zeros((2, 2, 2, 3, 2, 2, 2, 2, 64))
+    for delta in range(2):
+        for e in range(3):
+            for par in range(2):
+                for row in range(2):
+                    for jpar in range(2):
+                        for r4 in range(4):
+                            c, a = jpar + 2 * delta - par, r4 - row
+                            if 0 <= c < 3 and 0 <= a < 3:
+                                for o in range(2):
+                                    x = (9 * a + 3 * c + e) * 2 + o
+                                    pick[jpar, r4 // 2, delta, e, par, row, o, r4 % 2, x] = 1
+    return pick
 
 
 def constant_tables():
@@ -75,6 +102,9 @@
         "base": base,
         "gather": gather,
         "final": final,
+        "eye": np.eye(128),
+        "first": first_selection().reshape(4 * 64, 144),
+        "last": last_selection().reshape(4 * 48, 128),
     }
 
 
@@ -83,7 +113,7 @@
     where, parts, at = {}, [], 0
     for name, table in tables.items():
         where[name] = (at, table.shape[0])
-        parts.append(table)
+        parts.append(np.pad(table, ((0, 0), (0, 256 - table.shape[1]))))
         at += table.shape[0]
     return where, np.concatenate(parts, 0).astype(jnp.bfloat16)
 
@@ -91,51 +121,12 @@
 WHERE, TABLES = tables_array()
 
 
-def first_selection():
-    pick = np.zeros((4, 144, 54))
-    for j in range(4):
-        for a in range(3):
-            for e in range(3):
-                for c in range(2):
-                    for t in range(3):
-                        pick[j, ((a * 3 + e) * 2 + c) * 8 + j + t, (9 * a + 3 * t + e) * 2 + c] = 1
-    return pick
-
-
-def last_selection():
-    pick = np.zeros((24, 2, 4, 27))
-    for delta in range(2):
-        for e in range(3):
-            for par in range(2):
-                for row in range(2):
-                    for jpar in range(2):
-                        for r4 in range(4):
-                            c, a = jpar + 2 * delta - par, r4 - row
-                            if 0 <= c < 3 and 0 <= a < 3:
-                                pick[((delta * 3 + e) * 2 + par) * 2 + row, jpar, r4, 9 * a + 3 * c + e] = 1
-    return pick
-
-
-def prepared(first_w, time_w, last_w):
-    first = jnp.einsum(
-        "jkx,xo->jok", jnp.asarray(first_selection(), BF), first_w.reshape(54, 64), preferred_element_type=F32
-    )
-    first = first.reshape(256, 144).astype(BF)
-    turned = jnp.swapaxes(time_w, 1, 2)
-    eye, none = jnp.eye(64, dtype=BF), jnp.zeros((64, 64), BF)
-    time = jnp.concatenate(
-        [
-            jnp.concatenate([turned[1], turned[2], eye, none], 1),
-            jnp.concatenate([turned[0], turned[1], none, eye], 1),
-        ],
-        0,
-    )
-    last = jnp.einsum("mjrt,tio->mojri", jnp.asarray(last_selection(), BF), last_w, preferred_element_type=F32)
-    return first, time, last.reshape(48, 512).astype(BF)
-
-
 def dot(a, b):
     return jnp.dot(a, b, preferred_element_type=F32)
+
+
+def dot_turned(a, b):
+    return lax.dot_general(a, b, (((1,), (1,)), ((), ())), preferred_element_type=F32)
 
 
 def swap_blocks(x):
@@ -156,7 +147,7 @@
     tables_in, initial, coil_maps, kspace, sampled, first_in, time_in, last_in,
     out,
     tab, maps_raw, ksp_raw, img_raw, mask,
-    first_s, time_s, last_s,
+    first_r, time_r, last_r, first_s, time_s, last_s,
     maps_d, maps_w, ksp_d, img, acc, rs_send, rs_recv, halo, slab, total, outs,
     local_sem, core_send, core_recv, w_send, w_recv, rs_ssem, rs_rsem, h_ssem, h_rsem,
     ag_ssem, ag_rsem, o_ssem, o_rsem,
@@ -190,9 +181,9 @@
         local(2, kspace.at[block, :, :, core], ksp_raw.at[pl.ds(0, 2)]),
         local(3, sampled.at[:, :, core], mask.at[pl.ds(0, 2)]),
         local(4, initial.at[block, :, core], img_raw),
-        local(5, first_in, first_s.at[cas]),
-        local(6, time_in, time_s.at[cas]),
-        local(7, last_in, last_s.at[cas]),
+        local(5, first_in, first_r.at[cas]),
+        local(6, time_in, time_r.at[cas]),
+        local(7, last_in, last_r.at[cas]),
     ]
     for copy in loads:
         copy.start()
@@ -220,13 +211,13 @@
         copy.start()
     weights = [
         remote(source, target.at[cas], w_send.at[n], w_recv.at[n], other_cas)
-        for n, (source, target) in enumerate(((first_in, first_s), (time_in, time_s), (last_in, last_s)))
+        for n, (source, target) in enumerate(((first_in, first_r), (time_in, time_r), (last_in, last_r)))
     ]
     for copy in weights:
         copy.start()
     weights_in = [
         remote(source, target.at[1 - cas], w_send.at[n], w_recv.at[n], other_cas)
-        for n, (source, target) in enumerate(((first_in, first_s), (time_in, time_s), (last_in, last_s)))
+        for n, (source, target) in enumerate(((first_in, first_r), (time_in, time_r), (last_in, last_r)))
     ]
 
     zero_rows = jnp.zeros((2 * WIN, 256), BF)
@@ -325,6 +316,31 @@
         def _():
             to_after.start()
 
+    def weights_of(s):
+        @pl.when(cas != s)
+        def _():
+            for copy in weights_in:
+                copy.wait_recv()
+
+        eye = table("eye", 128)
+        small = table("eye", 64)[:64]
+        rows = dot_turned(small, first_r[s].reshape(54, 64)).astype(BF)
+        for j in range(4):
+            at = WHERE["first"][0] + 64 * j
+            first_s[64 * j:64 * j + 64] = dot(rows, tab[at:at + 54, :144]).astype(BF)
+        steps = time_r[s]
+        time_s[:64, :N] = dot_turned(small, steps[64:]).astype(BF)
+        time_s[64:, :N] = dot_turned(small, steps[:128]).astype(BF)
+        time_s[:, N:] = eye
+        taps = last_r[s].reshape(54, 64)
+        low, high = dot(taps, eye[:64]).astype(BF), dot(taps, eye[64:]).astype(BF)
+        lane = lax.broadcasted_iota(jnp.int32, (48, N), 1)
+        for n in range(4):
+            at = WHERE["last"][0] + 48 * n
+            part = dot(tab[at:at + 48, :54], low) + dot(tab[at:at + 48, 64:118], high)
+            edge = (lane < 64) & (ro == 0) if n % 2 == 0 else (lane >= 64) & (ro == 7)
+            last_s[:, N * n:N * n + N] = jnp.where(edge, 0.0, part)
+
     def denoise(s):
         for r in range(2):
             to_before, to_after = halo_copies(s, r)
@@ -347,26 +363,13 @@
                 for g in range(GROUPS):
                     slab[g, at:at + 16] = parts[16 * g:16 * g + 16]
 
-        if s == 0:
-            @pl.when(cas == 1)
-            def _():
-                for copy in weights_in:
-                    copy.wait_recv()
-        else:
-            @pl.when(cas == 0)
-            def _():
-                for copy in weights_in:
-                    copy.wait_recv()
-
-        row_of = (lax.broadcasted_iota(jnp.int32, (48, 512), 1) // 64) % 4
-        dead = ((row_of == 0) & (ro == 0)) | ((row_of == 3) & (ro == 7))
-        last = jnp.where(dead, 0.0, last_s[s].astype(F32))
         total[...] = jnp.zeros_like(total)
 
         def group(g, unused):
+            last = last_s[...]
             features = []
             for row in range(4):
-                hidden = dot(first_s[s], slab[g, 48 * row:48 * row + 144])
+                hidden = dot(first_s[...], slab[g, 48 * row:48 * row + 144])
                 hidden = jnp.maximum(hidden, 0.0).astype(BF)
                 for u in range(2):
                     lines = []
@@ -374,7 +377,7 @@
                         one = hidden[64 * j:64 * j + 64]
                         lines.append(jnp.concatenate([one[:, :N], one[:, N:]], 0))
                     lines = jnp.concatenate(lines, 1)
-                    mixed = dot(time_s[s], jnp.concatenate([lines, lines], 0))
+                    mixed = dot(time_s[...], jnp.concatenate([lines, lines], 0))
                     features.append(jnp.maximum(mixed, 0.0).astype(BF))
             for u in range(2):
                 k = 2 * g + u
@@ -462,6 +465,7 @@
     for s in range(2):
         data_consistency(s, 0)
         data_consistency(s, 1)
+        weights_of(s)
         combine(s, 0)
         combine(s, 1)
         image = denoise(s)
@@ -516,7 +520,6 @@
 
 
 def per_device(initial, coil_maps, kspace, sampled, first_w, time_w, last_w):
-    first, time, last = prepared(first_w[0], time_w[0], last_w[0])
     dma = pltpu.SemaphoreType.DMA
     out = pl.pallas_call(
         kernel,
@@ -529,9 +532,12 @@
             pltpu.VMEM((4, 2, 2, 256, N), BF),
             pltpu.VMEM((2, 2, 256, N), BF),
             pltpu.VMEM((4, 2, N, N), jnp.int32),
-            pltpu.VMEM((2, 256, 144), BF),
-            pltpu.VMEM((2, 128, 256), BF),
-            pltpu.VMEM((2, 48, 512), BF),
+            pltpu.VMEM((2, 27, 2, 64), BF),
+            pltpu.VMEM((2, 192, 64), BF),
+            pltpu.VMEM((2, 27, 2, 64), BF),
+            pltpu.VMEM((256, 144), BF),
+            pltpu.VMEM((128, 256), BF),
+            pltpu.VMEM((48, 512), F32),
             pltpu.VMEM((4, 256, 256), F32),
             pltpu.VMEM((4, 2 * ZS * WIN, 256), F32),
             pltpu.VMEM((4, 2, 256, 256), BF),
@@ -558,7 +564,7 @@
             dma((3,)),
         ],
         compiler_params=pltpu.CompilerParams(
-            collective_id=0, has_side_effects=True, vmem_limit_bytes=48 * 1024 * 1024
+            collective_id=0, has_side_effects=True, vmem_limit_bytes=60_000_000
         ),
     )(
         jnp.asarray(TABLES),
@@ -566,9 +572,9 @@
         coil_maps.reshape(2, 2, 2, 256, N),
         kspace.reshape(2, 2, 2, 2, 2, 256, N),
         sampled.reshape(2, 2, 2, N, N),
-        first,
-        time,
-        last,
+        first_w[0],
+        time_w[0].reshape(192, 64),
+        jnp.swapaxes(last_w[0], 1, 2),
     )
     return out.reshape(1, 2, 4, 2, 16, 2, N)
 

time: 70.3 us -> 59.5 us (0.85)
  local copies, waits for them, and re-layouts: 9.42 us -> 1.65 us
  matrix products: 2.08 us -> 0 us
    unnamed x14 -> x1, local copies, waits for them, and re-layouts: 8.49 us -> 1.65 us
    dot_general x2 -> x0, matrix products: 2.08 us -> none  [the longest x1 1.12 us: prepared(): jnp.einsum('jkx,xo->jok', jnp.asarray(first_selection(), BF), first_w.res...]
    another operation x1 -> x0, local copies, waits for them, and re-layouts: 0.74 us -> none  [prepared(): first_w.reshape(54, 64)]
where the time goes in v2:
time: 59.5 us; the launch traced here: 59.4 us
  Pallas kernels  57.7 us (97%)
  local copies, waits for them, and re-layouts  1.65 us (3%)
    pallas_call x1, Pallas kernels, per_device(): pl.pallas_call(kernel, out_shape=jax.ShapeDtypeStruct((2, 2, 2, 2, 32, N)...  57.7 us
    unnamed x1, local copies, waits for them, and re-layouts  1.65 us

profile of v2, /device:TPU:11, one launch (start us, length us, event | category | flops | bytes accessed | tf_op | source)
XLA Modules:
  0.0 59.4 jit_solution(11281214186079081294)
XLA Ops:
  0.0 57.7 %shard_map.82 = bf16[2,2,2,2,32,128]{5,4,3,2,1,0:T(8,128)(2,1)} custom-call(bf16[3280,256]{1,0:T(8,128)(2,1)} %constant.2.clone.tables_in, bf16[2,2,2,2,256,128]{5,4,3,2,1,0:T(8,128)(2,1)} %bitcast.11, bf16[2,2,2,256,128]{4,3,2,1,0:T(8,128)(2,1)} %bitcast.12, bf16[2,2,2,2,2,256,128]{6,5,4,3,2,1,0:T(8,128)(2,1)} %bitcast.10, s32[2,2,2,128,128]{4,3,2,1,0:T(8,128)} %bitcast.13, ...), custom_call_target="tpu_custom_call" | custom-call | tf_op jit(solution)/shard_map/pallas_call | solution.py:524
  57.7 1.7 %copy.10 = bf16[1,2,4,2,16,2,128]{6,5,4,3,2,1,0:T(2,128)(2,1)} copy(bf16[1,2,4,2,16,2,128]{6,5,4,3,2,1,0:T(2,128)(2,1)} %bitcast.14) | data formatting | bytes 262144

commit v3 on v2

v3 whole, which is shorter than its diff:
```python
import functools

import jax
import jax.numpy as jnp
import numpy as np
from jax import lax
from jax.experimental import pallas as pl
from jax.experimental.pallas import tpu as pltpu
from jax.sharding import PartitionSpec as P

MESH = pl.DeviceIdType.MESH
BF = jnp.bfloat16
F32 = jnp.float32
N = 128
ZS = 4
SHARE = N // ZS
WIN = 40
GROUPS = 9


def complex_blocks(direction):
    k = np.arange(N)
    angle = ((k[:, None] * k[None, :]) % N).astype(np.float32) * np.float32(2.0 * np.pi / N)
    factor = np.float32(1.0 / np.sqrt(N))
    cos, sin = np.cos(angle) * factor, direction * np.sin(angle) * factor
    return np.block([[cos, -sin], [sin, cos]]), np.block([[cos, sin], [-sin, cos]])


def first_selection():
    pick = np.zeros((4, 64, 144))
    for j in range(4):
        for a in range(3):
            for e in range(3):
                for c in range(2):
                    for t in range(3):
                        pick[j, (9 * a + 3 * t + e) * 2 + c, ((a * 3 + e) * 2 + c) * 8 + j + t] = 1
    return pick


def last_selection():
    pick = np.zeros((2, 3, 2, 3, 4, 2, 2, 64))
    for a in range(3):
        for delta in range(2):
            for e in range(3):
                for line in range(4):
                    for j in range(4):
                        c = j + 4 * delta - line
                        if 0 <= c < 3:
                            for o in range(2):
                                pick[j // 2, 2 - a, delta, e, line, o, j % 2, (9 * a + 3 * c + e) * 2 + o] = 1
    return pick


def constant_tables():
    rows_forward, cols_forward = complex_blocks(-1.0)
    rows_inverse, cols_inverse = complex_blocks(1.0)
    deint = np.zeros((256, 256))
    for c in range(2):
        for l in range(N):
            deint[c * N + l, 2 * l + c] = 1
    window = np.zeros((2 * ZS * WIN, 256))
    for c in range(2):
        for z in range(ZS):
            for w in range(SHARE + 4):
                l = SHARE * z - 2 + w
                if 0 <= l < N:
                    window[(c * ZS + z) * WIN + w, c * N + l] = 1
    shift = [np.zeros((256, 256)) for _ in range(2)]
    for q in range(2):
        for p in range(N):
            if p > 0:
                shift[0][q * N + p - 1, q * N + p] = 1
            if p < N - 1:
                shift[1][q * N + p + 1, q * N + p] = 1
    slabs = np.zeros((GROUPS * 16, 256))
    for g in range(GROUPS):
        for c in range(2):
            for l8 in range(8):
                slabs[g * 16 + c * 8 + l8, c * WIN + 4 * g + l8] = 1
    base = np.zeros((64, 256))
    gather = np.zeros((64, 256))
    for l in range(SHARE):
        for o in range(2):
            base[2 * l + o, o * WIN + 2 + l] = 1
            gather[o * SHARE + l, 2 * l + o] = 1
    return {
        "deint": deint,
        "deint_window": window @ deint,
        "rows_forward": rows_forward,
        "cols_forward": cols_forward,
        "cols_inverse": cols_inverse,
        "rows_inverse": window @ rows_inverse,
        "shift0": shift[0],
        "shift2": shift[1],
        "slabs": slabs,
        "base": base,
        "gather": gather,
        "eye": np.eye(128),
        "first": first_selection().reshape(4 * 64, 144),
        "last": last_selection().reshape(2 * 144, 128),
    }


def tables_array():
    tables = constant_tables()
    where, parts, at = {}, [], 0
    for name, table in tables.items():
        where[name] = (at, table.shape[0])
        parts.append(np.pad(table, ((0, 0), (0, 256 - table.shape[1]))))
        at += table.shape[0]
    return where, np.concatenate(parts, 0).astype(jnp.bfloat16)


WHERE, TABLES = tables_array()


def dot(a, b):
    return jnp.dot(a, b, preferred_element_type=F32)


def dot_turned(a, b):
    return lax.dot_general(a, b, (((1,), (1,)), ((), ())), preferred_element_type=F32)


def swap_blocks(x):
    return jnp.concatenate(
        [
            jnp.concatenate([x[:N, :N], x[N:, :N]], 1),
            jnp.concatenate([x[:N, N:], x[N:, N:]], 1),
        ],
        0,
    )


def twice(x):
    return jnp.concatenate([x, x], 1)


def kernel(
    tables_in, initial, coil_maps, kspace, sampled, first_in, time_in, last_in,
    out,
    tab, maps_raw, ksp_raw, img_raw, mask,
    first_r, time_r, last_r, first_s, time_s, last_s,
    maps_d, maps_w, ksp_d, img, acc, rs_send, rs_recv, halo, slab, total, outs,
    local_sem, core_send, core_recv, w_send, w_recv, rs_ssem, rs_rsem, h_ssem, h_rsem,
    ag_ssem, ag_rsem, o_ssem, o_rsem,
):
    cas, coil, ro = lax.axis_index("cascade"), lax.axis_index("coil"), lax.axis_index("readout")
    z, core = coil // 2, coil % 2
    hi = ro % 2
    block = 1 - (hi + cas - 2 * hi * cas)
    other_core = (cas, coil + 1 - 2 * core, ro)
    other_cas = (1 - cas, coil, ro)
    other_both = (1 - cas, coil + 1 - 2 * core, ro)
    peers = [(cas, 2 * ((z + d) % ZS) + core, ro) for d in (1, 2, 3)]
    before, after = (1 - cas, coil, ro - 1), (1 - cas, coil, ro + 1)
    has_before, has_after = ro > 0, ro < 7

    def table(name, columns=256):
        at, count = WHERE[name]
        return tab[at:at + count, :columns]

    def local(number, source, target):
        return pltpu.make_async_copy(source, target, local_sem.at[number])

    def remote(source, target, ssem, rsem, device):
        return pltpu.make_async_remote_copy(
            src_ref=source, dst_ref=target, send_sem=ssem, recv_sem=rsem, device_id=device, device_id_type=MESH
        )

    loads = [
        local(0, tables_in, tab),
        local(1, coil_maps.at[block], maps_raw.at[pl.ds(0, 2)]),
        local(2, kspace.at[block, :, :, core], ksp_raw.at[pl.ds(0, 2)]),
        local(3, sampled.at[:, :, core], mask.at[pl.ds(0, 2)]),
        local(4, initial.at[block, :, core], img_raw),
        local(5, first_in, first_r.at[cas]),
        local(6, time_in, time_r.at[cas]),
        local(7, last_in, last_r.at[cas]),
    ]
    for copy in loads:
        copy.start()

    barrier = pltpu.get_barrier_semaphore()
    for device in [other_core, other_cas, other_both, *peers]:
        pl.semaphore_signal(barrier, inc=1, device_id=device, device_id_type=MESH)

    @pl.when(has_before)
    def _():
        pl.semaphore_signal(barrier, inc=1, device_id=before, device_id_type=MESH)

    @pl.when(has_after)
    def _():
        pl.semaphore_signal(barrier, inc=1, device_id=after, device_id_type=MESH)

    exchange = [remote(sampled.at[:, :, 1 - core], mask.at[pl.ds(2, 2)], core_send.at[4], core_recv.at[4], other_core)]
    for r in range(2):
        exchange += [
            remote(
                kspace.at[block, :, :, 1 - core, r], ksp_raw.at[pl.ds(2, 2), :, r],
                core_send.at[2 * r], core_recv.at[2 * r], other_core,
            ),
            remote(
                coil_maps.at[block, :, r], maps_raw.at[pl.ds(2, 2), r],
                core_send.at[2 * r + 1], core_recv.at[2 * r + 1], other_core,
            ),
        ]
    weights = [
        remote(source, target.at[cas], w_send.at[n], w_recv.at[n], other_cas)
        for n, (source, target) in enumerate(((first_in, first_r), (time_in, time_r), (last_in, last_r)))
    ]
    weights_in = [
        remote(source, target.at[1 - cas], w_send.at[n], w_recv.at[n], other_cas)
        for n, (source, target) in enumerate(((first_in, first_r), (time_in, time_r), (last_in, last_r)))
    ]

    zero_rows = jnp.zeros((2 * WIN, 256), BF)
    for s in range(2):
        @pl.when(ro == 0)
        def _():
            halo[s, 0] = zero_rows
            halo[s, 1] = zero_rows

        @pl.when(ro == 7)
        def _():
            halo[s, 4] = zero_rows
            halo[s, 5] = zero_rows

    def prepare(pair, r):
        both = jnp.concatenate([maps_raw[2 * pair, r], maps_raw[2 * pair + 1, r]], 1)
        maps_d[pair, r] = dot(table("deint"), both)
        maps_w[pair, r] = dot(table("deint_window"), both)
        for j in (2 * pair, 2 * pair + 1):
            phases = jnp.concatenate([ksp_raw[j, 0, r], ksp_raw[j, 1, r]], 1)
            ksp_d[j, r] = swap_blocks(dot(table("deint"), phases)).astype(BF)

    def consistency(s, r, coils):
        image = img[s, r].astype(F32)
        real, imag = image[:, 0].reshape(N, 256), image[:, 1].reshape(N, 256)
        stage = []
        for j in coils:
            lanes = slice(j % 2 * N, j % 2 * N + N)
            map_r, map_i = twice(maps_d[j // 2, r, :N, lanes]), twice(maps_d[j // 2, r, N:, lanes])
            stage.append(jnp.concatenate([map_r * real - map_i * imag, map_r * imag + map_i * real], 0).astype(BF))
        forward = table("rows_forward")
        stage = [swap_blocks(dot(forward, x).astype(BF)) for x in stage]
        forward = table("cols_forward")
        stage = [dot(x, forward) for x in stage]
        stage = [
            jnp.where(twice(mask[j].reshape(256, N)) != 0, ksp_d[j, r].astype(F32), x).astype(BF)
            for j, x in zip(coils, stage)
        ]
        inverse = table("cols_inverse")
        stage = [swap_blocks(dot(x, inverse).astype(BF)) for x in stage]
        inverse = table("rows_inverse")
        stage = [dot(inverse, x) for x in stage]
        rows = ZS * WIN
        sum_r, sum_i = 0.0, 0.0
        for j, x in zip(coils, stage):
            value_r, value_i = x[:rows], x[rows:]
            lanes = slice(j % 2 * N, j % 2 * N + N)
            win_r, win_i = twice(maps_w[j // 2, r, :rows, lanes]), twice(maps_w[j // 2, r, rows:, lanes])
            sum_r = sum_r + win_r * value_r + win_i * value_i
            sum_i = sum_i + win_r * value_i - win_i * value_r
        return sum_r, sum_i

    def reduce_copies(s, r):
        return [
            remote(
                rs_send.at[s, r, (z + d) % ZS], rs_recv.at[s, r, d - 1],
                rs_ssem.at[s, r, d - 1], rs_rsem.at[s, r, d - 1], peers[d - 1],
            )
            for d in (1, 2, 3)
        ]

    def reduce_send(s, r, sum_r, sum_i):
        for share in range(ZS):
            at = share * WIN
            rs_send[s, r, share] = jnp.concatenate([sum_r[at:at + WIN], sum_i[at:at + WIN]], 0).astype(BF)
        for copy in reduce_copies(s, r):
            copy.start()

    def halo_copies(s, r):
        return (
            remote(halo.at[s, 2 + r], halo.at[s, 4 + r], h_ssem.at[s, r, 0], h_rsem.at[s, r, 0], before),
            remote(halo.at[s, 2 + r], halo.at[s, r], h_ssem.at[s, r, 1], h_rsem.at[s, r, 1], after),
        )

    def combine(s, r):
        for copy in reduce_copies(s, r):
            copy.wait_recv()
        summed = rs_send[s, r, z].astype(F32)
        for d in range(3):
            summed = summed + rs_recv[s, r, d].astype(F32)
        halo[s, 2 + r] = summed.astype(BF)
        to_before, to_after = halo_copies(s, r)

        @pl.when(has_before)
        def _():
            to_before.start()

        @pl.when(has_after)
        def _():
            to_after.start()

    def weights_of(s):
        @pl.when(cas != s)
        def _():
            for copy in weights_in:
                copy.wait_recv()

        eye = table("eye", 128)
        small = table("eye", 64)[:64]
        rows = dot_turned(small, first_r[s].reshape(54, 64)).astype(BF)
        for j in range(4):
            at = WHERE["first"][0] + 64 * j
            first_s[64 * j:64 * j + 64] = dot(rows, tab[at:at + 54, :144]).astype(BF)
        steps = time_r[s]
        time_s[:64, :N] = dot_turned(small, steps[64:]).astype(BF)
        time_s[64:, :N] = dot_turned(small, steps[:128]).astype(BF)
        time_s[:, N:] = eye
        taps = last_r[s].reshape(54, 64)
        low, high = dot(taps, eye[:64]).astype(BF), dot(taps, eye[64:]).astype(BF)
        parts = []
        for n in range(2):
            at = WHERE["last"][0] + 144 * n
            parts.append(dot(tab[at:at + 144, :54], low) + dot(tab[at:at + 144, 64:118], high))
        last = jnp.concatenate(parts, 1)
        line = lax.broadcasted_iota(jnp.int32, (144, 256), 1) // 64
        for place in range(3):
            mine = last
            if place == 0:
                mine = jnp.where((line == 0) & (z == 0), 0.0, last)
            if place == 2:
                mine = jnp.where((line > 0) & (z == ZS - 1), 0.0, last)
            last_s[place, :144] = mine.astype(BF)
            last_s[place, 144:192] = (mine[96:] * jnp.where(ro == 0, 0.0, 1.0)).astype(BF)
            last_s[place, 192:] = (mine[:48] * jnp.where(ro == 7, 0.0, 1.0)).astype(BF)

    def spread(s, rows):
        cells = [halo[s, row] for row in rows]
        for e in range(3):
            moved = cells if e == 1 else [dot(x, table(f"shift{e}")).astype(BF) for x in cells]
            for row, x in zip(rows, moved):
                parts = dot(table("slabs", 2 * WIN), x).astype(BF)
                at = (row * 3 + e) * 16
                for g in range(GROUPS):
                    slab[g, at:at + 16] = parts[16 * g:16 * g + 16]

    def features(row, groups):
        weight = first_s[...]
        stage = [jnp.maximum(dot(weight, slab[g, 48 * row:48 * row + 144]), 0.0).astype(BF) for g in groups]
        columns = []
        for hidden in stage:
            for u in range(2):
                lines = []
                for j in (2 * u, 2 * u + 1):
                    one = hidden[64 * j:64 * j + 64]
                    lines.append(jnp.concatenate([one[:, :N], one[:, N:]], 0))
                lines = jnp.concatenate(lines, 1)
                columns.append(jnp.concatenate([lines, lines], 0))
        weight = time_s[...]
        columns = [jnp.maximum(dot(weight, x), 0.0).astype(BF) for x in columns]
        low, high = {0: (144, 192), 1: (48, 144), 2: (0, 96), 3: (192, 240)}[row]
        results = []
        for n, g in enumerate(groups):
            stack = []
            for u in range(2):
                for j in range(2):
                    one = columns[2 * n + u][:, j * N:j * N + N]
                    stack.append(jnp.concatenate([one[:64], one[64:]], 1))
            place = jnp.where(g == 0, 0, jnp.where(g == GROUPS - 1, 2, 1))
            results.append(dot(last_s[place, low:high], jnp.concatenate(stack, 0)))
        for n, target in enumerate({0: (0,), 1: (0, 1), 2: (0, 1), 3: (1,)}[row]):
            here = [x[48 * n:48 * n + 24] for x in results]
            left = [x[48 * n + 24:48 * n + 48] for x in results]
            total[target, groups[0]] += left[0]
            total[target, groups[1]] += here[0] + left[1]
            total[target, groups[2]] += here[1] + left[2]
            total[target, groups[2] + 1] += here[2]

    def sweep(rows):
        def some(it, unused):
            for row in rows:
                features(row, [3 * it, 3 * it + 1, 3 * it + 2])
            return unused

        lax.fori_loop(0, GROUPS // 3, some, 0)

    def halo_wait(s, r):
        to_before, to_after = halo_copies(s, r)

        @pl.when(has_after)
        def _():
            to_before.wait_recv()

        @pl.when(has_before)
        def _():
            to_after.wait_recv()

    def finish(s, r):
        taps = [total[r, 1:9, 8 * e:8 * e + 8].reshape(64, 256) for e in range(3)]
        lane = lax.broadcasted_iota(jnp.int32, (64, N), 1)
        halves = []
        for q in range(2):
            at = slice(q * N, q * N + N)
            low = jnp.where(lane == 0, 0.0, pltpu.roll(taps[0][:, at], 1, 1))
            high = jnp.where(lane == N - 1, 0.0, pltpu.roll(taps[2][:, at], N - 1, 1))
            halves.append(low + taps[1][:, at] + high)
        image = (dot(table("base", 2 * WIN), halo[s, 2 + r]) + jnp.concatenate(halves, 1)).astype(BF)
        if s == 0:
            share = dot(table("gather", 64), image).astype(BF)
            for c in range(2):
                img[1, r, z, c] = share[c * SHARE:c * SHARE + SHARE]
            for copy in gather_copies(r, False):
                copy.start()
        for half in range(2):
            for q in range(2):
                outs[s, r, half, q] = image[32 * half:32 * half + 32, q * N:q * N + N]
        send_output(s, r)

    def gather_copies(r, arriving):
        return [
            remote(
                img.at[1, r, z], img.at[1, r, (z + ZS - d) % ZS if arriving else z],
                ag_ssem.at[r, d - 1], ag_rsem.at[r, d - 1], peers[d - 1],
            )
            for d in (1, 2, 3)
        ]

    def near_copies(s, r):
        return (
            local(8 + r, outs.at[s, r, core], out.at[block, :, core, r]),
            remote(outs.at[s, r, 1 - core], out.at[block, :, core, r], o_ssem.at[r, 0], o_rsem.at[r, 0], other_core),
        )

    def far_copies(s, r):
        return (
            remote(outs.at[s, r, core], out.at[block, :, core, r], o_ssem.at[r, 1], o_rsem.at[r, 1], other_cas),
            remote(outs.at[s, r, 1 - core], out.at[block, :, core, r], o_ssem.at[r, 2], o_rsem.at[r, 2], other_both),
        )

    def send_output(s, r):
        @pl.when(cas == s)
        def _():
            for copy in near_copies(s, r):
                copy.start()

        @pl.when(cas != s)
        def _():
            for copy in far_copies(s, r):
                copy.start()

    for copy in loads[:5]:
        copy.wait()
    for r in range(2):
        phases = jnp.concatenate([img_raw[0, r], img_raw[1, r]], 1)
        plain = dot(table("deint"), phases).astype(BF)
        for share in range(ZS):
            for c in range(2):
                at = c * N + share * SHARE
                img[0, r, share, c] = plain[at:at + SHARE]
        prepare(0, r)
    for copy in loads[5:]:
        copy.wait()
    acc[0, 0], acc[0, 1] = consistency(0, 0, (0, 1))

    pl.semaphore_wait(barrier, 6 + jnp.where(has_before, 1, 0) + jnp.where(has_after, 1, 0))
    for copy in exchange + weights:
        copy.start()
    acc[1, 0], acc[1, 1] = consistency(0, 1, (0, 1))
    exchange[0].wait_recv()
    for r in range(2):
        for copy in exchange[1 + 2 * r:3 + 2 * r]:
            copy.wait_recv()
        prepare(1, r)
        sum_r, sum_i = consistency(0, r, (2, 3))
        reduce_send(0, r, acc[r, 0] + sum_r, acc[r, 1] + sum_i)

    for s in range(2):
        if s == 1:
            for r in range(2):
                for copy in gather_copies(r, True):
                    copy.wait_recv()
                reduce_send(1, r, *consistency(1, r, (0, 1, 2, 3)))
        weights_of(s)
        total[...] = jnp.zeros_like(total)
        combine(s, 0)
        spread(s, (2,))
        combine(s, 1)
        spread(s, (3,))
        halo_wait(s, 0)
        spread(s, (0, 4))
        sweep((2,))
        halo_wait(s, 1)
        spread(s, (1, 5))
        sweep((1, 0))
        finish(s, 0)
        sweep((3,))
        finish(s, 1)

    for copy in exchange + weights + gather_copies(0, False) + gather_copies(1, False):
        copy.wait_send()
    for s in range(2):
        for r in range(2):
            for copy in reduce_copies(s, r):
                copy.wait_send()
            to_before, to_after = halo_copies(s, r)

            @pl.when(has_before)
            def _():
                to_before.wait_send()

            @pl.when(has_after)
            def _():
                to_after.wait_send()

            @pl.when(cas == s)
            def _():
                keep, give = near_copies(s, r)
                keep.wait()
                give.wait_send()

            @pl.when(cas != s)
            def _():
                for copy in far_copies(s, r):
                    copy.wait_send()

    for r in range(2):
        source = outs.at[0, r, 0]
        arriving = (
            remote(source, out.at[block, :, 1 - core, r], o_ssem.at[r, 0], o_rsem.at[r, 0], other_core),
            remote(source, out.at[1 - block, :, core, r], o_ssem.at[r, 1], o_rsem.at[r, 1], other_cas),
            remote(source, out.at[1 - block, :, 1 - core, r], o_ssem.at[r, 2], o_rsem.at[r, 2], other_both),
        )
        for copy in arriving:
            copy.wait_recv()


def per_device(initial, coil_maps, kspace, sampled, first_w, time_w, last_w):
    dma = pltpu.SemaphoreType.DMA
    out = pl.pallas_call(
        kernel,
        out_shape=jax.ShapeDtypeStruct((2, 2, 2, 2, 32, N), BF),
        in_specs=[pl.BlockSpec(memory_space=pl.ANY)] * 8,
        out_specs=pl.BlockSpec(memory_space=pl.ANY),
        scratch_shapes=[
            pltpu.VMEM(TABLES.shape, BF),
            pltpu.VMEM((4, 2, 256, N), BF),
            pltpu.VMEM((4, 2, 2, 256, N), BF),
            pltpu.VMEM((2, 2, 256, N), BF),
            pltpu.VMEM((4, 2, N, N), jnp.int32),
            pltpu.VMEM((2, 27, 2, 64), BF),
            pltpu.VMEM((2, 192, 64), BF),
            pltpu.VMEM((2, 27, 2, 64), BF),
            pltpu.VMEM((256, 144), BF),
            pltpu.VMEM((128, 256), BF),
            pltpu.VMEM((3, 240, 256), BF),
            pltpu.VMEM((2, 2, 256, 256), F32),
            pltpu.VMEM((2, 2, 2 * ZS * WIN, 256), F32),
            pltpu.VMEM((4, 2, 256, 256), BF),
            pltpu.VMEM((2, 2, ZS, 2, SHARE, 256), BF),
            pltpu.VMEM((2, 2, ZS * WIN, 256), F32),
            pltpu.VMEM((2, 2, ZS, 2 * WIN, 256), BF),
            pltpu.VMEM((2, 2, 3, 2 * WIN, 256), BF),
            pltpu.VMEM((2, 6, 2 * WIN, 256), BF),
            pltpu.VMEM((GROUPS, 288, 256), BF),
            pltpu.VMEM((2, 10, 24, 256), F32),
            pltpu.VMEM((2, 2, 2, 2, 32, N), BF),
            dma((10,)),
            dma((5,)),
            dma((5,)),
            dma((3,)),
            dma((3,)),
            dma((2, 2, 3)),
            dma((2, 2, 3)),
            dma((2, 2, 2)),
            dma((2, 2, 2)),
            dma((2, 3)),
            dma((2, 3)),
            dma((2, 3)),
            dma((2, 3)),
        ],
        compiler_params=pltpu.CompilerParams(
            collective_id=0, has_side_effects=True, vmem_limit_bytes=60_000_000
        ),
    )(
        jnp.asarray(TABLES),
        initial.reshape(2, 2, 2, 2, 256, N),
        coil_maps.reshape(2, 2, 2, 256, N),
        kspace.reshape(2, 2, 2, 2, 2, 256, N),
        sampled.reshape(2, 2, 2, N, N),
        first_w[0],
        time_w[0].reshape(192, 64),
        jnp.swapaxes(last_w[0], 1, 2),
    )
    return out.reshape(1, 2, 4, 2, 16, 2, N)


def solution(mesh):
    in_specs = (
        P(None, None, "readout", None, None, None),
        P(None, "coil", "readout", None, None, None),
        P(None, "coil", None, "readout", None, None, None),
        P("coil", None, None, None),
        P("cascade", None, None, None),
        P("cascade", None, None, None),
        P("cascade", None, None, None),
    )
    out_specs = P("cascade", None, None, "readout", "coil", None, None)
    return jax.shard_map(per_device, mesh=mesh, in_specs=in_specs, out_specs=out_specs, check_vma=False)
```

time: 59.5 us -> 51.9 us (0.87)
  Pallas kernels: 57.7 us -> 50 us
    pallas_call x1, Pallas kernels: 57.7 us -> 50 us  [per_device(): pl.pallas_call(kernel, out_shape=jax.ShapeDtypeStruct((2, 2, 2, 2, 32, N)...]
where the time goes in v3:
time: 51.9 us; the launch traced here: 51.6 us
  Pallas kernels  50 us (96%)
  local copies, waits for them, and re-layouts  1.65 us (3%)
    pallas_call x1, Pallas kernels, per_device(): pl.pallas_call(kernel, out_shape=jax.ShapeDtypeStruct((2, 2, 2, 2, 32, N)...  50 us
    unnamed x1, local copies, waits for them, and re-layouts  1.65 us

profile of v3, /device:TPU:11, one launch (start us, length us, event | category | flops | bytes accessed | tf_op | source)
XLA Modules:
  0.0 51.6 jit_solution(16241616952166362364)
XLA Ops:
  0.0 50.0 %shard_map.82 = bf16[2,2,2,2,32,128]{5,4,3,2,1,0:T(8,128)(2,1)} custom-call(bf16[3120,256]{1,0:T(8,128)(2,1)} %constant.2.clone.tables_in, bf16[2,2,2,2,256,128]{5,4,3,2,1,0:T(8,128)(2,1)} %bitcast.11, bf16[2,2,2,256,128]{4,3,2,1,0:T(8,128)(2,1)} %bitcast.12, bf16[2,2,2,2,2,256,128]{6,5,4,3,2,1,0:T(8,128)(2,1)} %bitcast.10, s32[2,2,2,128,128]{4,3,2,1,0:T(8,128)} %bitcast.13, ...), custom_call_target="tpu_custom_call" | custom-call | tf_op jit(solution)/shard_map/pallas_call | solution.py:542
  50.0 1.7 %copy.10 = bf16[1,2,4,2,16,2,128]{6,5,4,3,2,1,0:T(2,128)(2,1)} copy(bf16[1,2,4,2,16,2,128]{6,5,4,3,2,1,0:T(2,128)(2,1)} %bitcast.14) | data formatting | bytes 262144

commit v4 on v3

--- a/solution.py
+++ b/solution.py
@@ -15,6 +15,7 @@
 ZS = 4
 SHARE = N // ZS
 WIN = 40
+LAG = 3
 GROUPS = 9
 
 
@@ -112,6 +113,8 @@
 
 
 WHERE, TABLES = tables_array()
+EARLY = sum(WHERE[name][1] for name in ("deint", "deint_window"))
+LATE = TABLES.shape[0] - EARLY
 
 
 def dot(a, b):
@@ -169,11 +172,12 @@
         )
 
     loads = [
-        local(0, tables_in, tab),
+        local(0, tables_in.at[pl.ds(0, EARLY)], tab.at[pl.ds(0, EARLY)]),
         local(1, coil_maps.at[block], maps_raw.at[pl.ds(0, 2)]),
         local(2, kspace.at[block, :, :, core], ksp_raw.at[pl.ds(0, 2)]),
+        local(4, initial.at[block, :, core], img_raw),
         local(3, sampled.at[:, :, core], mask.at[pl.ds(0, 2)]),
-        local(4, initial.at[block, :, core], img_raw),
+        local(10, tables_in.at[pl.ds(EARLY, LATE)], tab.at[pl.ds(EARLY, LATE)]),
         local(5, first_in, first_r.at[cas]),
         local(6, time_in, time_r.at[cas]),
         local(7, last_in, last_r.at[cas]),
@@ -347,45 +351,44 @@
                 for g in range(GROUPS):
                     slab[g, at:at + 16] = parts[16 * g:16 * g + 16]
 
-    def features(row, groups):
-        weight = first_s[...]
-        stage = [jnp.maximum(dot(weight, slab[g, 48 * row:48 * row + 144]), 0.0).astype(BF) for g in groups]
+    def lifted(row, g):
+        return jnp.maximum(dot(first_s[...], slab[g, 48 * row:48 * row + 144]), 0.0).astype(BF)
+
+    def in_time(hidden):
         columns = []
-        for hidden in stage:
-            for u in range(2):
-                lines = []
-                for j in (2 * u, 2 * u + 1):
-                    one = hidden[64 * j:64 * j + 64]
-                    lines.append(jnp.concatenate([one[:, :N], one[:, N:]], 0))
-                lines = jnp.concatenate(lines, 1)
-                columns.append(jnp.concatenate([lines, lines], 0))
-        weight = time_s[...]
-        columns = [jnp.maximum(dot(weight, x), 0.0).astype(BF) for x in columns]
+        for u in range(2):
+            lines = []
+            for j in (2 * u, 2 * u + 1):
+                one = hidden[64 * j:64 * j + 64]
+                lines.append(jnp.concatenate([one[:, :N], one[:, N:]], 0))
+            lines = jnp.concatenate(lines, 1)
+            columns.append(lines)
+        weight = time_s[:, :N]
+        columns = [jnp.maximum(dot(weight, x) + x.astype(F32), 0.0).astype(BF) for x in columns]
+        stack = []
+        for u in range(2):
+            for j in range(2):
+                one = columns[u][:, j * N:j * N + N]
+                stack.append(jnp.concatenate([one[:64], one[64:]], 1))
+        return jnp.concatenate(stack, 0)
+
+    def projected(row, g, stack):
         low, high = {0: (144, 192), 1: (48, 144), 2: (0, 96), 3: (192, 240)}[row]
-        results = []
-        for n, g in enumerate(groups):
-            stack = []
-            for u in range(2):
-                for j in range(2):
-                    one = columns[2 * n + u][:, j * N:j * N + N]
-                    stack.append(jnp.concatenate([one[:64], one[64:]], 1))
-            place = jnp.where(g == 0, 0, jnp.where(g == GROUPS - 1, 2, 1))
-            results.append(dot(last_s[place, low:high], jnp.concatenate(stack, 0)))
+        result = dot(last_s[0 if g == 0 else 2 if g == GROUPS - 1 else 1, low:high], stack)
         for n, target in enumerate({0: (0,), 1: (0, 1), 2: (0, 1), 3: (1,)}[row]):
-            here = [x[48 * n:48 * n + 24] for x in results]
-            left = [x[48 * n + 24:48 * n + 48] for x in results]
-            total[target, groups[0]] += left[0]
-            total[target, groups[1]] += here[0] + left[1]
-            total[target, groups[2]] += here[1] + left[2]
-            total[target, groups[2] + 1] += here[2]
+            total[target, g + 1] += result[48 * n:48 * n + 24]
+            total[target, g] += result[48 * n + 24:48 * n + 48]
 
     def sweep(rows):
-        def some(it, unused):
-            for row in rows:
-                features(row, [3 * it, 3 * it + 1, 3 * it + 2])
-            return unused
-
-        lax.fori_loop(0, GROUPS // 3, some, 0)
+        units = [(row, g) for g in range(GROUPS) for row in rows]
+        hidden, stacks = {}, {}
+        for n in range(len(units) + 2 * LAG):
+            if n < len(units):
+                hidden[n] = lifted(*units[n])
+            if 0 <= n - LAG < len(units):
+                stacks[n - LAG] = in_time(hidden.pop(n - LAG))
+            if 0 <= n - 2 * LAG:
+                projected(*units[n - 2 * LAG], stacks.pop(n - 2 * LAG))
 
     def halo_wait(s, r):
         to_before, to_after = halo_copies(s, r)
@@ -451,7 +454,10 @@
             for copy in far_copies(s, r):
                 copy.start()
 
-    for copy in loads[:5]:
+    pl.semaphore_wait(barrier, 6 + jnp.where(has_before, 1, 0) + jnp.where(has_after, 1, 0))
+    for copy in exchange + weights:
+        copy.start()
+    for copy in loads[:4]:
         copy.wait()
     for r in range(2):
         phases = jnp.concatenate([img_raw[0, r], img_raw[1, r]], 1)
@@ -461,13 +467,10 @@
                 at = c * N + share * SHARE
                 img[0, r, share, c] = plain[at:at + SHARE]
         prepare(0, r)
-    for copy in loads[5:]:
+    for copy in loads[4:]:
         copy.wait()
     acc[0, 0], acc[0, 1] = consistency(0, 0, (0, 1))
 
-    pl.semaphore_wait(barrier, 6 + jnp.where(has_before, 1, 0) + jnp.where(has_after, 1, 0))
-    for copy in exchange + weights:
-        copy.start()
     acc[1, 0], acc[1, 1] = consistency(0, 1, (0, 1))
     exchange[0].wait_recv()
     for r in range(2):
@@ -567,7 +570,7 @@
             pltpu.VMEM((GROUPS, 288, 256), BF),
             pltpu.VMEM((2, 10, 24, 256), F32),
             pltpu.VMEM((2, 2, 2, 2, 32, N), BF),
-            dma((10,)),
+            dma((11,)),
             dma((5,)),
             dma((5,)),
             dma((3,)),

time: 51.9 us -> 45.4 us (0.87)
  Pallas kernels: 50 us -> 43.6 us
    pallas_call x1, Pallas kernels: 50 us -> 43.6 us  [per_device(): pl.pallas_call(kernel, out_shape=jax.ShapeDtypeStruct((2, 2, 2, 2, 32, N)...]
where the time goes in v4:
time: 45.4 us; the launch traced here: 45.3 us
  Pallas kernels  43.6 us (96%)
  local copies, waits for them, and re-layouts  1.65 us (4%)
    pallas_call x1, Pallas kernels, per_device(): pl.pallas_call(kernel, out_shape=jax.ShapeDtypeStruct((2, 2, 2, 2, 32, N)...  43.6 us
    unnamed x1, local copies, waits for them, and re-layouts  1.65 us

profile of v4, /device:TPU:11, one launch (start us, length us, event | category | flops | bytes accessed | tf_op | source)
XLA Modules:
  0.0 45.3 jit_solution(7918096453704510884)
XLA Ops:
  0.0 43.6 %shard_map.82 = bf16[2,2,2,2,32,128]{5,4,3,2,1,0:T(8,128)(2,1)} custom-call(bf16[3120,256]{1,0:T(8,128)(2,1)} %constant.2.clone.tables_in, bf16[2,2,2,2,256,128]{5,4,3,2,1,0:T(8,128)(2,1)} %bitcast.11, bf16[2,2,2,256,128]{4,3,2,1,0:T(8,128)(2,1)} %bitcast.12, bf16[2,2,2,2,2,256,128]{6,5,4,3,2,1,0:T(8,128)(2,1)} %bitcast.10, s32[2,2,2,128,128]{4,3,2,1,0:T(8,128)} %bitcast.13, ...), custom_call_target="tpu_custom_call" | custom-call | tf_op jit(solution)/shard_map/pallas_call | solution.py:545
  43.6 1.7 %copy.10 = bf16[1,2,4,2,16,2,128]{6,5,4,3,2,1,0:T(2,128)(2,1)} copy(bf16[1,2,4,2,16,2,128]{6,5,4,3,2,1,0:T(2,128)(2,1)} %bitcast.14) | data formatting | bytes 262144

commit v5 on v4

--- a/solution.py
+++ b/solution.py
@@ -34,7 +34,8 @@
             for e in range(3):
                 for c in range(2):
                     for t in range(3):
-                        pick[j, (9 * a + 3 * t + e) * 2 + c, ((a * 3 + e) * 2 + c) * 8 + j + t] = 1
+                        at = (a * 3 + e) * 16 + (j + t) // 4 * 8 + c * 4 + (j + t) % 4
+                        pick[j, (9 * a + 3 * t + e) * 2 + c, at] = 1
     return pick
 
 
@@ -66,23 +67,11 @@
                 l = SHARE * z - 2 + w
                 if 0 <= l < N:
                     window[(c * ZS + z) * WIN + w, c * N + l] = 1
-    shift = [np.zeros((256, 256)) for _ in range(2)]
-    for q in range(2):
-        for p in range(N):
-            if p > 0:
-                shift[0][q * N + p - 1, q * N + p] = 1
-            if p < N - 1:
-                shift[1][q * N + p + 1, q * N + p] = 1
-    slabs = np.zeros((GROUPS * 16, 256))
-    for g in range(GROUPS):
-        for c in range(2):
-            for l8 in range(8):
-                slabs[g * 16 + c * 8 + l8, c * WIN + 4 * g + l8] = 1
     base = np.zeros((64, 256))
     gather = np.zeros((64, 256))
     for l in range(SHARE):
         for o in range(2):
-            base[2 * l + o, o * WIN + 2 + l] = 1
+            base[2 * l + o, (l + 2) // 4 * 8 + o * 4 + (l + 2) % 4] = 1
             gather[o * SHARE + l, 2 * l + o] = 1
     return {
         "deint": deint,
@@ -91,9 +80,6 @@
         "cols_forward": cols_forward,
         "cols_inverse": cols_inverse,
         "rows_inverse": window @ rows_inverse,
-        "shift0": shift[0],
-        "shift2": shift[1],
-        "slabs": slabs,
         "base": base,
         "gather": gather,
         "eye": np.eye(128),
@@ -296,7 +282,13 @@
         summed = rs_send[s, r, z].astype(F32)
         for d in range(3):
             summed = summed + rs_recv[s, r, d].astype(F32)
-        halo[s, 2 + r] = summed.astype(BF)
+        top = lax.broadcasted_iota(jnp.int32, (8, 256), 0) < 4
+        parts = []
+        for at in range(0, WIN, 8):
+            real, imag = summed[at:at + 8], summed[WIN + at:WIN + at + 8]
+            parts.append(jnp.where(top, real, pltpu.roll(imag, 4, 0)))
+            parts.append(jnp.where(top, pltpu.roll(real, 4, 0), imag))
+        halo[s, 2 + r] = jnp.concatenate(parts, 0).astype(BF)
         to_before, to_after = halo_copies(s, r)
 
         @pl.when(has_before)
@@ -341,15 +333,19 @@
             last_s[place, 144:192] = (mine[96:] * jnp.where(ro == 0, 0.0, 1.0)).astype(BF)
             last_s[place, 192:] = (mine[:48] * jnp.where(ro == 7, 0.0, 1.0)).astype(BF)
 
+    def moved(x, by):
+        lane = lax.broadcasted_iota(jnp.int32, (x.shape[0], N), 1)
+        dead = lane == (0 if by == 1 else N - 1)
+        halves = [pltpu.roll(x[:, at:at + N], by % N, 1) for at in (0, N)]
+        return jnp.concatenate([jnp.where(dead, 0.0, half) for half in halves], 1)
+
     def spread(s, rows):
-        cells = [halo[s, row] for row in rows]
-        for e in range(3):
-            moved = cells if e == 1 else [dot(x, table(f"shift{e}")).astype(BF) for x in cells]
-            for row, x in zip(rows, moved):
-                parts = dot(table("slabs", 2 * WIN), x).astype(BF)
+        for row in rows:
+            cells = halo[s, row].astype(F32)
+            for e, x in enumerate((moved(cells, 1), cells, moved(cells, -1))):
                 at = (row * 3 + e) * 16
                 for g in range(GROUPS):
-                    slab[g, at:at + 16] = parts[16 * g:16 * g + 16]
+                    slab[g, at:at + 16] = x[8 * g:8 * g + 16].astype(BF)
 
     def lifted(row, g):
         return jnp.maximum(dot(first_s[...], slab[g, 48 * row:48 * row + 144]), 0.0).astype(BF)
@@ -403,14 +399,8 @@
 
     def finish(s, r):
         taps = [total[r, 1:9, 8 * e:8 * e + 8].reshape(64, 256) for e in range(3)]
-        lane = lax.broadcasted_iota(jnp.int32, (64, N), 1)
-        halves = []
-        for q in range(2):
-            at = slice(q * N, q * N + N)
-            low = jnp.where(lane == 0, 0.0, pltpu.roll(taps[0][:, at], 1, 1))
-            high = jnp.where(lane == N - 1, 0.0, pltpu.roll(taps[2][:, at], N - 1, 1))
-            halves.append(low + taps[1][:, at] + high)
-        image = (dot(table("base", 2 * WIN), halo[s, 2 + r]) + jnp.concatenate(halves, 1)).astype(BF)
+        change = moved(taps[0], 1) + taps[1] + moved(taps[2], -1)
+        image = (dot(table("base", 2 * WIN), halo[s, 2 + r]) + change).astype(BF)
         if s == 0:
             share = dot(table("gather", 64), image).astype(BF)
             for c in range(2):

time: 45.4 us -> 44.1 us (0.971)
  Pallas kernels: 43.6 us -> 42.3 us
    pallas_call x1, Pallas kernels: 43.6 us -> 42.3 us  [per_device(): pl.pallas_call(kernel, out_shape=jax.ShapeDtypeStruct((2, 2, 2, 2, 32, N)...]
where the time goes in v5:
time: 44.1 us; the launch traced here: 44 us
  Pallas kernels  42.3 us (96%)
  local copies, waits for them, and re-layouts  1.65 us (4%)
    pallas_call x1, Pallas kernels, per_device(): pl.pallas_call(kernel, out_shape=jax.ShapeDtypeStruct((2, 2, 2, 2, 32, N)...  42.3 us
    unnamed x1, local copies, waits for them, and re-layouts  1.65 us

profile of v5, /device:TPU:11, one launch (start us, length us, event | category | flops | bytes accessed | tf_op | source)
XLA Modules:
  0.0 44.0 jit_solution(394464906769258285)
XLA Ops:
  0.0 42.3 %shard_map.82 = bf16[2,2,2,2,32,128]{5,4,3,2,1,0:T(8,128)(2,1)} custom-call(bf16[2464,256]{1,0:T(8,128)(2,1)} %constant.2.clone.tables_in, bf16[2,2,2,2,256,128]{5,4,3,2,1,0:T(8,128)(2,1)} %bitcast.11, bf16[2,2,2,256,128]{4,3,2,1,0:T(8,128)(2,1)} %bitcast.12, bf16[2,2,2,2,2,256,128]{6,5,4,3,2,1,0:T(8,128)(2,1)} %bitcast.10, s32[2,2,2,128,128]{4,3,2,1,0:T(8,128)} %bitcast.13, ...), custom_call_target="tpu_custom_call" | custom-call | tf_op jit(solution)/shard_map/pallas_call | solution.py:535
  42.3 1.7 %copy.10 = bf16[1,2,4,2,16,2,128]{6,5,4,3,2,1,0:T(2,128)(2,1)} copy(bf16[1,2,4,2,16,2,128]{6,5,4,3,2,1,0:T(2,128)(2,1)} %bitcast.14) | data formatting | bytes 262144

commit v6 on v5

--- a/solution.py
+++ b/solution.py
@@ -157,6 +157,18 @@
             src_ref=source, dst_ref=target, send_sem=ssem, recv_sem=rsem, device_id=device, device_id_type=MESH
         )
 
+    barrier = pltpu.get_barrier_semaphore()
+    for device in [other_core, other_cas, other_both, *peers]:
+        pl.semaphore_signal(barrier, inc=1, device_id=device, device_id_type=MESH)
+
+    @pl.when(has_before)
+    def _():
+        pl.semaphore_signal(barrier, inc=1, device_id=before, device_id_type=MESH)
+
+    @pl.when(has_after)
+    def _():
+        pl.semaphore_signal(barrier, inc=1, device_id=after, device_id_type=MESH)
+
     loads = [
         local(0, tables_in.at[pl.ds(0, EARLY)], tab.at[pl.ds(0, EARLY)]),
         local(1, coil_maps.at[block], maps_raw.at[pl.ds(0, 2)]),
@@ -170,18 +182,6 @@
     ]
     for copy in loads:
         copy.start()
-
-    barrier = pltpu.get_barrier_semaphore()
-    for device in [other_core, other_cas, other_both, *peers]:
-        pl.semaphore_signal(barrier, inc=1, device_id=device, device_id_type=MESH)
-
-    @pl.when(has_before)
-    def _():
-        pl.semaphore_signal(barrier, inc=1, device_id=before, device_id_type=MESH)
-
-    @pl.when(has_after)
-    def _():
-        pl.semaphore_signal(barrier, inc=1, device_id=after, device_id_type=MESH)
 
     exchange = [remote(sampled.at[:, :, 1 - core], mask.at[pl.ds(2, 2)], core_send.at[4], core_recv.at[4], other_core)]
     for r in range(2):
@@ -410,7 +410,8 @@
         for half in range(2):
             for q in range(2):
                 outs[s, r, half, q] = image[32 * half:32 * half + 32, q * N:q * N + N]
-        send_output(s, r)
+        if s == 1:
+            send_output(s, r)
 
     def gather_copies(r, arriving):
         return [
@@ -476,6 +477,8 @@
                 for copy in gather_copies(r, True):
                     copy.wait_recv()
                 reduce_send(1, r, *consistency(1, r, (0, 1, 2, 3)))
+            send_output(0, 0)
+            send_output(0, 1)
         weights_of(s)
         total[...] = jnp.zeros_like(total)
         combine(s, 0)

time: 44.1 us -> 44 us (level)
  no operation moved by 1% of the time
where the time goes in v6:
time: 44 us; the launch traced here: 43.9 us
  Pallas kernels  42.2 us (96%)
  local copies, waits for them, and re-layouts  1.65 us (4%)
    pallas_call x1, Pallas kernels, per_device(): pl.pallas_call(kernel, out_shape=jax.ShapeDtypeStruct((2, 2, 2, 2, 32, N)...  42.2 us
    unnamed x1, local copies, waits for them, and re-layouts  1.65 us

profile of v6, /device:TPU:11, one launch (start us, length us, event | category | flops | bytes accessed | tf_op | source)
XLA Modules:
  0.0 43.9 jit_solution(2867024150632520751)
XLA Ops:
  0.0 42.2 %shard_map.82 = bf16[2,2,2,2,32,128]{5,4,3,2,1,0:T(8,128)(2,1)} custom-call(bf16[2464,256]{1,0:T(8,128)(2,1)} %constant.2.clone.tables_in, bf16[2,2,2,2,256,128]{5,4,3,2,1,0:T(8,128)(2,1)} %bitcast.11, bf16[2,2,2,256,128]{4,3,2,1,0:T(8,128)(2,1)} %bitcast.12, bf16[2,2,2,2,2,256,128]{6,5,4,3,2,1,0:T(8,128)(2,1)} %bitcast.10, s32[2,2,2,128,128]{4,3,2,1,0:T(8,128)} %bitcast.13, ...), custom_call_target="tpu_custom_call" | custom-call | tf_op jit(solution)/shard_map/pallas_call | solution.py:538
  42.2 1.7 %copy.10 = bf16[1,2,4,2,16,2,128]{6,5,4,3,2,1,0:T(2,128)(2,1)} copy(bf16[1,2,4,2,16,2,128]{6,5,4,3,2,1,0:T(2,128)(2,1)} %bitcast.14) | data formatting | bytes 262144

commit v7 on v6

--- a/solution.py
+++ b/solution.py
@@ -128,7 +128,7 @@
 def kernel(
     tables_in, initial, coil_maps, kspace, sampled, first_in, time_in, last_in,
     out,
-    tab, maps_raw, ksp_raw, img_raw, mask,
+    tab, maps_raw, ksp_raw, img_raw, mask_raw, mask_send, mask,
     first_r, time_r, last_r, first_s, time_s, last_s,
     maps_d, maps_w, ksp_d, img, acc, rs_send, rs_recv, halo, slab, total, outs,
     local_sem, core_send, core_recv, w_send, w_recv, rs_ssem, rs_rsem, h_ssem, h_rsem,
@@ -170,11 +170,11 @@
         pl.semaphore_signal(barrier, inc=1, device_id=after, device_id_type=MESH)
 
     loads = [
+        local(3, sampled, mask_raw),
         local(0, tables_in.at[pl.ds(0, EARLY)], tab.at[pl.ds(0, EARLY)]),
         local(1, coil_maps.at[block], maps_raw.at[pl.ds(0, 2)]),
         local(2, kspace.at[block, :, :, core], ksp_raw.at[pl.ds(0, 2)]),
         local(4, initial.at[block, :, core], img_raw),
-        local(3, sampled.at[:, :, core], mask.at[pl.ds(0, 2)]),
         local(10, tables_in.at[pl.ds(EARLY, LATE)], tab.at[pl.ds(EARLY, LATE)]),
         local(5, first_in, first_r.at[cas]),
         local(6, time_in, time_r.at[cas]),
@@ -183,7 +183,7 @@
     for copy in loads:
         copy.start()
 
-    exchange = [remote(sampled.at[:, :, 1 - core], mask.at[pl.ds(2, 2)], core_send.at[4], core_recv.at[4], other_core)]
+    exchange = [remote(mask_send, mask.at[pl.ds(2, 2)], core_send.at[4], core_recv.at[4], other_core)]
     for r in range(2):
         exchange += [
             remote(
@@ -237,7 +237,7 @@
         forward = table("cols_forward")
         stage = [dot(x, forward) for x in stage]
         stage = [
-            jnp.where(twice(mask[j].reshape(256, N)) != 0, ksp_d[j, r].astype(F32), x).astype(BF)
+            jnp.where(twice(mask[j].reshape(256, N).astype(F32)) > 0.5, ksp_d[j, r].astype(F32), x).astype(BF)
             for j, x in zip(coils, stage)
         ]
         inverse = table("cols_inverse")
@@ -445,10 +445,15 @@
             for copy in far_copies(s, r):
                 copy.start()
 
+    loads[0].wait()
+    for j in range(2):
+        for q in range(2):
+            mask[j, q] = mask_raw[j, q, core].astype(F32).astype(BF)
+            mask_send[j, q] = mask_raw[j, q, 1 - core].astype(F32).astype(BF)
     pl.semaphore_wait(barrier, 6 + jnp.where(has_before, 1, 0) + jnp.where(has_after, 1, 0))
     for copy in exchange + weights:
         copy.start()
-    for copy in loads[:4]:
+    for copy in loads[1:5]:
         copy.wait()
     for r in range(2):
         phases = jnp.concatenate([img_raw[0, r], img_raw[1, r]], 1)
@@ -458,7 +463,7 @@
                 at = c * N + share * SHARE
                 img[0, r, share, c] = plain[at:at + SHARE]
         prepare(0, r)
-    for copy in loads[4:]:
+    for copy in loads[5:]:
         copy.wait()
     acc[0, 0], acc[0, 1] = consistency(0, 0, (0, 1))
 
@@ -545,7 +550,9 @@
             pltpu.VMEM((4, 2, 256, N), BF),
             pltpu.VMEM((4, 2, 2, 256, N), BF),
             pltpu.VMEM((2, 2, 256, N), BF),
-            pltpu.VMEM((4, 2, N, N), jnp.int32),
+            pltpu.VMEM((2, 2, 2, N, N), jnp.int32),
+            pltpu.VMEM((2, 2, N, N), BF),
+            pltpu.VMEM((4, 2, N, N), BF),
             pltpu.VMEM((2, 27, 2, 64), BF),
             pltpu.VMEM((2, 192, 64), BF),
             pltpu.VMEM((2, 27, 2, 64), BF),

time: 44 us -> 44.7 us (1.016)
  Pallas kernels: 42.2 us -> 42.9 us
    pallas_call x1, Pallas kernels: 42.2 us -> 42.9 us  [per_device(): pl.pallas_call(kernel, out_shape=jax.ShapeDtypeStruct((2, 2, 2, 2, 32, N)...]
where the time goes in v7:
time: 44.7 us; the launch traced here: 44.6 us
  Pallas kernels  42.9 us (96%)
  local copies, waits for them, and re-layouts  1.65 us (4%)
    pallas_call x1, Pallas kernels, per_device(): pl.pallas_call(kernel, out_shape=jax.ShapeDtypeStruct((2, 2, 2, 2, 32, N)...  42.9 us
    unnamed x1, local copies, waits for them, and re-layouts  1.65 us

profile of v7, /device:TPU:11, one launch (start us, length us, event | category | flops | bytes accessed | tf_op | source)
XLA Modules:
  0.0 44.6 jit_solution(11482512704429907301)
XLA Ops:
  0.0 42.9 %shard_map.82 = bf16[2,2,2,2,32,128]{5,4,3,2,1,0:T(8,128)(2,1)} custom-call(bf16[2464,256]{1,0:T(8,128)(2,1)} %constant.2.clone.tables_in, bf16[2,2,2,2,256,128]{5,4,3,2,1,0:T(8,128)(2,1)} %bitcast.11, bf16[2,2,2,256,128]{4,3,2,1,0:T(8,128)(2,1)} %bitcast.12, bf16[2,2,2,2,2,256,128]{6,5,4,3,2,1,0:T(8,128)(2,1)} %bitcast.10, s32[2,2,2,128,128]{4,3,2,1,0:T(8,128)} %bitcast.13, ...), custom_call_target="tpu_custom_call" | custom-call | tf_op jit(solution)/shard_map/pallas_call | solution.py:543
  42.9 1.7 %copy.10 = bf16[1,2,4,2,16,2,128]{6,5,4,3,2,1,0:T(2,128)(2,1)} copy(bf16[1,2,4,2,16,2,128]{6,5,4,3,2,1,0:T(2,128)(2,1)} %bitcast.14) | data formatting | bytes 262144

commit v8 on v6

--- a/solution.py
+++ b/solution.py
@@ -386,16 +386,15 @@
             if 0 <= n - 2 * LAG:
                 projected(*units[n - 2 * LAG], stacks.pop(n - 2 * LAG))
 
-    def halo_wait(s, r):
-        to_before, to_after = halo_copies(s, r)
-
+    def wait_after(s, r):
         @pl.when(has_after)
         def _():
-            to_before.wait_recv()
-
+            halo_copies(s, r)[0].wait_recv()
+
+    def wait_before(s, r):
         @pl.when(has_before)
         def _():
-            to_after.wait_recv()
+            halo_copies(s, r)[1].wait_recv()
 
     def finish(s, r):
         taps = [total[r, 1:9, 8 * e:8 * e + 8].reshape(64, 256) for e in range(3)]
@@ -485,11 +484,13 @@
         spread(s, (2,))
         combine(s, 1)
         spread(s, (3,))
-        halo_wait(s, 0)
-        spread(s, (0, 4))
+        wait_after(s, 0)
+        spread(s, (4,))
         sweep((2,))
-        halo_wait(s, 1)
-        spread(s, (1, 5))
+        wait_before(s, 0)
+        wait_before(s, 1)
+        wait_after(s, 1)
+        spread(s, (0, 1, 5))
         sweep((1, 0))
         finish(s, 0)
         sweep((3,))

time: 44 us -> 44 us (level)
  no operation moved by 1% of the time
where the time goes in v8:
time: 44 us; the launch traced here: 43.9 us
  Pallas kernels  42.2 us (96%)
  local copies, waits for them, and re-layouts  1.65 us (4%)
    pallas_call x1, Pallas kernels, per_device(): pl.pallas_call(kernel, out_shape=jax.ShapeDtypeStruct((2, 2, 2, 2, 32, N)...  42.2 us
    unnamed x1, local copies, waits for them, and re-layouts  1.65 us

profile of v8, /device:TPU:11, one launch (start us, length us, event | category | flops | bytes accessed | tf_op | source)
XLA Modules:
  0.0 43.9 jit_solution(4578984198711401631)
XLA Ops:
  0.0 42.2 %shard_map.82 = bf16[2,2,2,2,32,128]{5,4,3,2,1,0:T(8,128)(2,1)} custom-call(bf16[2464,256]{1,0:T(8,128)(2,1)} %constant.2.clone.tables_in, bf16[2,2,2,2,256,128]{5,4,3,2,1,0:T(8,128)(2,1)} %bitcast.11, bf16[2,2,2,256,128]{4,3,2,1,0:T(8,128)(2,1)} %bitcast.12, bf16[2,2,2,2,2,256,128]{6,5,4,3,2,1,0:T(8,128)(2,1)} %bitcast.10, s32[2,2,2,128,128]{4,3,2,1,0:T(8,128)} %bitcast.13, ...), custom_call_target="tpu_custom_call" | custom-call | tf_op jit(solution)/shard_map/pallas_call | solution.py:539
  42.2 1.7 %copy.10 = bf16[1,2,4,2,16,2,128]{6,5,4,3,2,1,0:T(2,128)(2,1)} copy(bf16[1,2,4,2,16,2,128]{6,5,4,3,2,1,0:T(2,128)(2,1)} %bitcast.14) | data formatting | bytes 262144
